TPU v7x, 768 devices: a whole 4x8x12 slice. The times are simulated.
768 devices in a mesh: dp: 4 (over x), expert: 48 (over z, y_lo), tensor: 4 (over y_hi, core).
Axes of the slice: x: 4, y: 8 (y_hi: 2, y_lo: 4; y = y_hi * 4 + y_lo), z: 12, core: 2. Of those that a mesh axis runs over, the one named last changes fastest.
Arguments:
- grad_out: bfloat16 [24576, 4096], P(('dp', 'expert')), may hold values from -6 to 6
- expert_ids: int32 [24576, 8], P(('dp', 'expert')), may hold values from 0 to 127, all different within a row
- gate_values: bfloat16 [24576, 8], P(('dp', 'expert')), may hold values from 0.019897461 to 0.5
- saved_hidden: bfloat16 [4, 48, 192, 1536], P('dp', 'expert', None, 'tensor'), may hold values from -0.59765625 to 0.59765625
- down_weight: bfloat16 [48, 1536, 4096], P('expert', 'tensor'), may hold values from -0.15625 to 0.15625
Outputs:
- gate_grad: float32 [24576, 8], P(('dp', 'expert'))
- hidden_grad: bfloat16 [4, 48, 192, 1536], P('dp', 'expert', None, 'tensor')
- down_grad: float32 [48, 1536, 4096], P('expert', 'tensor', 'dp')
Inputs may be any that keep to these rules, and one draw needn't show every extreme that they name: `expert_ids`: the 8 experts of a row differ.
All inputs are finite; a program needn't handle non-finite values.
Results may differ from a plain program's by a relative error of at most 0.0085.
Values may be sent and summed in bfloat16 or wider, within the bound.
A program may use at most 32 MiB of HBM per device.

v0:
```python
import jax
import jax.numpy as jnp
from jax import lax
from jax.sharding import PartitionSpec as P

CAP = 4


def slot_table(route_ids, gate_rows, count):
    experts = jnp.arange(count, dtype=jnp.int32)
    hits = (route_ids[:, :, None] == experts[None, None, :]).astype(jnp.int32)
    member = jnp.sum(hits, axis=1)
    gate_expert = jnp.sum(
        jnp.where(hits > 0, gate_rows.astype(jnp.float32)[:, :, None], 0.0), axis=1
    )
    before = jnp.cumsum(member, axis=0) - member
    kept = member * (before < CAP).astype(jnp.int32)
    places = jnp.arange(CAP, dtype=jnp.int32)
    match = kept.T[:, None, :] * (before.T[:, None, :] == places[None, :, None]).astype(jnp.int32)
    positions = jnp.arange(route_ids.shape[0], dtype=jnp.int32)
    source_row = jnp.sum(match * positions[None, None, :], axis=2)
    filled = jnp.sum(match, axis=2)
    slot_gate = jnp.sum(match.astype(jnp.float32) * gate_expert.T[:, None, :], axis=2).astype(
        jnp.bfloat16
    )
    return (source_row, filled, slot_gate, hits, kept, before)


def returned_grad(back, hits, kept, before):
    count = back.shape[0]
    spots = jnp.minimum(before, CAP - 1)
    picked = back[jnp.arange(count, dtype=jnp.int32)[None, :], spots]
    picked = jnp.where(kept > 0, picked, jnp.zeros((), picked.dtype))
    return jnp.sum(hits.astype(picked.dtype) * picked[:, None, :], axis=2)


def on_device(grad_out, expert_ids, gate_values, saved_hidden, down_weight):
    count = lax.axis_size("expert")
    source_row, filled, slot_gate, hits, kept, before = slot_table(expert_ids, gate_values, count)
    outgoing = jnp.where(
        filled[:, :, None] > 0, grad_out[source_row], jnp.zeros((), grad_out.dtype)
    )
    arrived, gate_in = (
        lax.all_to_all(outgoing, "expert", split_axis=0, concat_axis=0, tiled=True),
        lax.all_to_all(slot_gate, "expert", split_axis=0, concat_axis=0, tiled=True),
    )
    slot_count = count * CAP
    arrived = arrived.reshape(slot_count, grad_out.shape[1])
    gate_column = gate_in.reshape(slot_count, 1).astype(jnp.float32)
    weight = down_weight[0]
    hidden = saved_hidden[0, 0]
    upstream = lax.dot_general(
        arrived, weight, (((1,), (1,)), ((), ())), preferred_element_type=jnp.float32
    )
    hidden_grad = (gate_column * upstream).astype(jnp.bfloat16)
    gate_part = jnp.sum(hidden.astype(jnp.float32) * upstream, axis=1)
    gate_total = lax.psum(gate_part, "tensor")
    back = lax.all_to_all(
        gate_total.reshape(count, CAP), "expert", split_axis=0, concat_axis=0, tiled=True
    )
    weighted = (gate_column * arrived.astype(jnp.float32)).astype(jnp.bfloat16)
    summed = lax.psum_scatter(
        lax.dot_general(
            weighted, hidden, (((0,), (0,)), ((), ())), preferred_element_type=jnp.float32
        ).astype(jnp.bfloat16),
        "dp",
        scatter_dimension=0,
        tiled=True,
    ).astype(jnp.float32)
    down_grad = summed.T[None]
    gate_grad = returned_grad(back, hits, kept, before)
    return (gate_grad, hidden_grad[None, None], down_grad)


def solution(mesh):
    return jax.shard_map(
        on_device,
        mesh=mesh,
        in_specs=(
            P(("dp", "expert"), None),
            P(("dp", "expert"), None),
            P(("dp", "expert"), None),
            P("dp", "expert", None, "tensor"),
            P("expert", "tensor", None),
        ),
        out_specs=(
            P(("dp", "expert"), None),
            P("dp", "expert", None, "tensor"),
            P("expert", "tensor", "dp"),
        ),
        check_vma=False,
    )
```

profile of v0, /device:TPU:1, one launch (start us, length us, event | category | flops | bytes accessed | tf_op | source)
XLA Modules:
  0.0 294.1 jit_solution(3826111092044637614)
XLA Ops:
  7.2 0.0 copy-start
  7.2 0.9 convert_reduce_fusion
  8.0 0.1 copy.31
  8.1 0.2 reduce_window_sum.13
  8.3 0.0 copy-start.1
  8.3 0.1 copy.36
  8.4 0.0 copy-start.2
  8.4 0.1 copy.35
  8.5 0.0 copy-start.3
  8.5 0.2 select_reduce_fusion.1
  8.7 0.1 copy.37
  8.9 0.1 copy.38
  8.9 0.1 reshape.111
  9.1 5.6 %gather_fusion = bf16[192,4096]{1,0:T(8,128)(2,1)} fusion(bf16[128,4096]{1,0:T(8,128)(2,1)} %param.5, s32[1024]{0:T(1024)S(1)} %pad_clamp_fusion), kind=kCustom, calls=%fused_computation | custom fusion | bytes 3146496 | tf_op jit(solution)/shard_map/gather | solution.py:41
  14.6 0.0 copy-done.1
  14.6 0.0 copy-done.2
  14.6 0.0 copy-done.3
  14.6 3.7 %reshape.110 = bf16[48,4,4096]{2,1,0:T(4,128)(2,1)} reshape(bf16[192,4096]{1,0:T(8,128)(2,1)} %gather_fusion) | data formatting | bytes 3145728 | tf_op jit(solution)/shard_map/gather | solution.py:41
  18.3 2.2 broadcast_select_fusion
  20.4 75.3 %all_to_all.23 = bf16[48,4,4096]{2,1,0:T(4,128)(2,1)} all-to-all(bf16[48,4,4096]{2,1,0:T(4,128)(2,1)S(1)} %broadcast_select_fusion), channel_id=1, replica_groups=mesh['dp'=4,'expert'=48,'tensor'=4] {'expert'}, dimensions={0} | all-to-all | bytes 3145728 | tf_op jit(solution)/shard_map/all_to_all | solution.py:44
  95.8 3.5 %reshape.105 = bf16[192,4096]{1,0:T(8,128)(2,1)} reshape(bf16[48,4,4096]{2,1,0:T(4,128)(2,1)} %all_to_all.23) | data formatting | bytes 3145728 | tf_op jit(solution)/shard_map/reshape | solution.py:48
  99.2 0.0 copy-done
  99.2 0.0 copy-start.4
  99.3 2.7 multiply_reduce_fusion
  102.0 0.1 all_to_all.16
  102.1 21.0 %psum.7 = f32[48,1,4]{2,0,1:T(8,128)} all-reduce(f32[48,1,4]{2,0,1:T(8,128)S(1)} %all_to_all.16), channel_id=1, replica_groups=mesh['dp'=4,'expert'=48,'tensor'=4] {'tensor'}, use_global_device_ids=true, to_apply=%region_5.6 | all-reduce | flops 192 | bytes 1536 | tf_op jit(solution)/shard_map/psum | solution.py:57
  123.0 6.3 %all-to-all-start.1 = ((f32[48,1,4]{2,1,0:T(1,128)}), f32[48,1,4]{2,1,0:T(1,128)S(1)}, u32[]{:S(2)}, u32[]{:S(2)}) async-start(f32[48,1,4]{2,1,0:T(1,128)} %bitcast.5), calls=%async_computation.1 | async-start | bytes 49152 | tf_op jit(solution)/shard_map/all_to_all | solution.py:58
  129.3 0.0 reduce-scatter.2.cloned.1.call-start
  129.4 1.5 fusion.11
  130.9 0.0 copy-done.4
  130.9 0.6 convert_element_type.68
  131.5 0.9 reshape.117
  132.4 8.1 %all-to-all-done.1 = f32[48,1,4]{2,1,0:T(1,128)S(1)} async-done(((f32[48,1,4]{2,1,0:T(1,128)}), f32[48,1,4]{2,1,0:T(1,128)S(1)}, u32[]{:S(2)}, u32[]{:S(2)}) %all-to-all-start.1) | async-done | bytes 800 | tf_op jit(solution)/shard_map/all_to_all | solution.py:58
  140.5 66.0 %gather_fusion.1 = f32[6144]{0:T(1024)} fusion(f32[48,4]{1,0:T(8,128)S(1)} %bitcast.39, s32[6144]{0:T(1024)S(1)} %reshape.117), kind=kCustom, calls=%fused_computation.1 | custom fusion | bytes 98304 | tf_op jit(solution)/shard_map/gather | solution.py:32
  206.5 1.4 reshape.120
  207.9 1.5 fusion.12
  209.4 0.9 copy.40
  210.3 1.4 select_reduce_fusion
  211.7 0.9 fusion.8
  212.5 0.1 copy.41
  212.7 15.1 %all_to_all.24 = bf16[48,1,4]{2,1,0:T(2,128)(2,1)S(1)} all-to-all(bf16[48,1,4]{2,1,0:T(2,128)(2,1)S(1)} %copy.41), channel_id=1, replica_groups=mesh['dp'=4,'expert'=48,'tensor'=4] {'expert'}, dimensions={0} | all-to-all | bytes 768 | tf_op jit(solution)/shard_map/all_to_all | solution.py:45
  227.8 3.9 %multiply_convert_fusion = bf16[48,4,4096]{2,1,0:T(4,128)(2,1)} fusion(bf16[48,4,4096]{2,1,0:T(4,128)(2,1)} %all_to_all.23, f32[48,4]{1,0:T(8,128)S(1)} %bitcast.40), kind=kLoop, calls=%fused_computation.5 | loop fusion | flops 2359296 | bytes 3146496 | tf_op jit(solution)/shard_map/convert_element_type | solution.py:61
  231.6 3.5 %convert_element_type.78 = bf16[192,4096]{1,0:T(8,128)(2,1)} reshape(bf16[48,4,4096]{2,1,0:T(4,128)(2,1)} %multiply_convert_fusion) | data formatting | bytes 3145728 | tf_op jit(solution)/shard_map/convert_element_type | solution.py:61
  235.1 4.4 %convolution_convert_fusion = bf16[4096,384]{1,0:T(8,128)(2,1)} fusion(bf16[192,4096]{1,0:T(8,128)(2,1)} %convert_element_type.78, bf16[1,1,192,384]{3,2,1,0:T(8,128)(2,1)} %param.8), kind=kOutput, calls=%fused_computation.2 | convolution fusion | flops 605552640 | bytes 4866048 | tf_op jit(solution)/shard_map/dot_general | solution.py:63
  239.5 0.0 reduce-scatter.2.cloned.1.call-update
  239.6 0.1 convert_reduce_fusion.1
  239.6 0.1 reshape.106
  239.7 0.8 fusion.4
  240.5 41.3 %reduce-scatter.2.cloned.1.call-done = bf16[1024,384]{1,0:T(8,128)(2,1)} async-done(((bf16[4096,384]{1,0:T(8,128)(2,1)}), bf16[1024,384]{1,0:T(8,128)(2,1)}) %reduce-scatter.2.cloned.1.call-update) | async-done | bytes 786448 | tf_op jit(solution)/shard_map/reduce_scatter | solution.py:62
  281.8 2.4 convert_bitcast_fusion
  284.2 3.0 %copy.42 = f32[1,384,1024]{2,1,0:T(8,128)} copy(f32[1,384,1024]{1,2,0:T(8,128)} %convert_bitcast_fusion) | data formatting | bytes 3145728
  (5 shorter events, 0.1 us)
Async XLA Ops:
  7.2 92.1 %copy-start = (bf16[1,384,4096]{2,1,0:T(8,128)(2,1)S(1)}, bf16[1,384,4096]{2,1,0:T(8,128)(2,1)}, u32[]{:S(2)}) copy-start(bf16[1,384,4096]{2,1,0:T(8,128)(2,1)} %param.9) | copy-start | bytes 9437188
  8.3 6.3 %copy-start.1 = (s32[128,48]{1,0:T(8,128)}, s32[128,48]{1,0:T(8,128)S(1)}, u32[]{:S(2)}) copy-start(s32[128,48]{1,0:T(8,128)S(1)} %reduce_window_sum.13) | copy-start | bytes 73732
  8.4 6.2 %copy-start.2 = (s32[48,128]{1,0:T(8,128)}, s32[48,128]{1,0:T(8,128)S(1)}, u32[]{:S(2)}) copy-start(s32[48,128]{1,0:T(8,128)S(1)} %copy.36) | copy-start | bytes 73732
  8.5 6.1 %copy-start.3 = (s32[48,128]{1,0:T(8,128)}, s32[48,128]{1,0:T(8,128)S(1)}, u32[]{:S(2)}) copy-start(s32[48,128]{1,0:T(8,128)S(1)} %copy.35) | copy-start | bytes 73732
  99.2 31.6 %copy-start.4 = (bf16[128,8]{0,1:T(8,128)(2,1)S(1)}, bf16[128,8]{0,1:T(8,128)(2,1)}, u32[]{:S(2)}) copy-start(bf16[128,8]{0,1:T(8,128)(2,1)} %param.7) | copy-start | bytes 6148
  123.0 17.5 %all-to-all-start.1 = ((f32[48,1,4]{2,1,0:T(1,128)}), f32[48,1,4]{2,1,0:T(1,128)S(1)}, u32[]{:S(2)}, u32[]{:S(2)}) async-start(f32[48,1,4]{2,1,0:T(1,128)} %bitcast.5), calls=%async_computation.1 | async-start | bytes 49152 | tf_op jit(solution)/shard_map/all_to_all | solution.py:58
  129.3 152.5 %reduce-scatter.2.cloned.1.call-start = ((), (), s32[]{:S(2)}) async-start(), calls=%async_computation.4 | async-start | bytes 3932160 | tf_op jit(solution)/shard_map/reduce_scatter | solution.py:62
Sparse Core Ops, SparseCore 0:
  239.7 42.1 reduce-scatter.1
where the time goes:
time: 295 us; the launch traced here: 294 us
  blocking collectives  111 us (38%)
  local copies, waits for them, and re-layouts  89.3 us (30%)
  waiting for transfers between devices  49.5 us (17%)
  other arithmetic  16.4 us (6%)
  between operations  14.1 us (5%)
  matrix products  7.09 us (2%)
  starting transfers between devices  6.32 us (2%)
    all_to_all x1, blocking collectives, on_device(): lax.all_to_all(outgoing, 'expert', split_axis=0, concat_axis=0, tiled=True)  75.3 us
    gather x2, local copies, waits for them, and re-layouts, returned_grad(): picked = back[jnp.arange(count, dtype=jnp.int32)[None, :], spots]  67.4 us
    reduce_scatter x1, waiting for transfers between devices, on_device(): lax.psum_scatter(lax.dot_general(weighted, hidden, (((0,), (0,)), ((), ()...  41.3 us
    psum x1, blocking collectives, on_device(): gate_total = lax.psum(gate_part, 'tensor')  21 us
    all_to_all x1, blocking collectives, on_device(): lax.all_to_all(slot_gate, 'expert', split_axis=0, concat_axis=0, tiled=True)  15.1 us
    gather x2, local copies, waits for them, and re-layouts, on_device(): grad_out[source_row]  9.21 us
    all_to_all x1, waiting for transfers between devices, on_device(): lax.all_to_all(gate_total.reshape(count, CAP), 'expert', split_axis=0, co...  8.11 us
    all_to_all x1, starting transfers between devices, on_device(): lax.all_to_all(gate_total.reshape(count, CAP), 'expert', split_axis=0, co...  6.28 us
  transfers between devices with their start and end apart: 2, of which 2 were waited for; matrix products, arithmetic and copies ran while one was open for 1% of the time, Pallas kernels for 0%

commit v1 on v0

v1 whole, which is shorter than its diff:
```python
import jax
import jax.numpy as jnp
from jax import lax
from jax.sharding import PartitionSpec as P

CAP = 4


def on_device(grad_out, expert_ids, gate_values, saved_hidden, down_weight):
    count = lax.axis_size("expert")
    tokens, top = expert_ids.shape
    width = grad_out.shape[1]
    slot_count = count * CAP
    ids = expert_ids.T
    gates = gate_values.T.astype(jnp.float32)
    experts = jnp.arange(count, dtype=jnp.int32)
    hits = ids[:, None, :] == experts[None, :, None]
    member = jnp.sum(hits.astype(jnp.float32), axis=0)
    gate_expert = jnp.sum(jnp.where(hits, gates[:, None, :], 0.0), axis=0)
    order = jnp.arange(tokens, dtype=jnp.int32)
    earlier = (order[:, None] < order[None, :]).astype(jnp.bfloat16)
    before = lax.dot_general(
        member.astype(jnp.bfloat16), earlier, (((1,), (0,)), ((), ())),
        preferred_element_type=jnp.float32,
    )
    places = jnp.arange(CAP, dtype=jnp.float32)
    match = (member[:, None, :] > 0) & (before[:, None, :] == places[None, :, None])
    slot_gate = jnp.sum(jnp.where(match, gate_expert[:, None, :], 0.0), axis=2)
    pick = match.astype(jnp.bfloat16).reshape(slot_count, tokens)
    outgoing = lax.dot_general(
        pick, grad_out, (((1,), (0,)), ((), ())), preferred_element_type=jnp.float32
    ).astype(jnp.bfloat16)
    tail = jnp.broadcast_to(
        slot_gate.astype(jnp.bfloat16).reshape(slot_count, 1), (slot_count, 128)
    )
    payload = jnp.concatenate([outgoing, tail], axis=1).reshape(count, CAP, width + 128)
    landed = lax.all_to_all(payload, "expert", split_axis=0, concat_axis=0, tiled=True)
    landed = landed.reshape(slot_count, width + 128)
    arrived = landed[:, :width]
    gate_column = landed[:, width:width + 1].astype(jnp.float32)
    weight = down_weight[0]
    hidden = saved_hidden[0, 0]
    scaled = (gate_column * hidden.astype(jnp.float32)).astype(jnp.bfloat16)
    summed = lax.psum_scatter(
        lax.dot_general(
            arrived, scaled, (((0,), (0,)), ((), ())), preferred_element_type=jnp.float32
        ).astype(jnp.bfloat16),
        "dp", scatter_dimension=0, tiled=True,
    )
    upstream = lax.dot_general(
        arrived, weight, (((1,), (1,)), ((), ())), preferred_element_type=jnp.float32
    )
    hidden_grad = (gate_column * upstream).astype(jnp.bfloat16)
    gate_part = jnp.sum(hidden.astype(jnp.float32) * upstream, axis=1)
    gate_total = lax.psum(gate_part, "tensor")
    back = lax.all_to_all(
        gate_total.reshape(count, CAP), "expert", split_axis=0, concat_axis=0, tiled=True
    )
    picked = jnp.sum(jnp.where(match, back[:, :, None], 0.0), axis=1)
    gate_grad = jnp.sum(jnp.where(hits, picked[None], 0.0), axis=1).T
    down_grad = summed.astype(jnp.float32).T[None]
    return (gate_grad, hidden_grad[None, None], down_grad)


def solution(mesh):
    return jax.shard_map(
        on_device,
        mesh=mesh,
        in_specs=(
            P(("dp", "expert"), None),
            P(("dp", "expert"), None),
            P(("dp", "expert"), None),
            P("dp", "expert", None, "tensor"),
            P("expert", "tensor", None),
        ),
        out_specs=(
            P(("dp", "expert"), None),
            P("dp", "expert", None, "tensor"),
            P("expert", "tensor", "dp"),
        ),
        check_vma=False,
    )
```

time: 295 us -> 160 us (0.54)
  local copies, waits for them, and re-layouts: 89.3 us -> 10.6 us
  waiting for transfers between devices: 49.5 us -> 1.45 us
  other arithmetic: 16.4 us -> 7.13 us
  starting transfers between devices: 6.32 us -> 0.04 us
  blocking collectives: 111 us -> 115 us
    gather x4 -> x0, local copies, waits for them, and re-layouts: 76.6 us -> none  [the longest x2 67.4 us: returned_grad(): picked = back[jnp.arange(count, dtype=jnp.int32)[None, :], spots]]
    reduce_scatter x1, waiting for transfers between devices: 41.3 us -> 1.43 us  [on_device(): lax.psum_scatter(lax.dot_general(arrived, scaled, (((0,), (0,)), ((), ())...]
    all_to_all x1 -> x0, waiting for transfers between devices: 8.11 us -> none  [on_device(): lax.all_to_all(gate_total.reshape(count, CAP), 'expert', split_axis=0, co...]
    all_to_all x1 -> x0, starting transfers between devices: 6.28 us -> none  [on_device(): lax.all_to_all(gate_total.reshape(count, CAP), 'expert', split_axis=0, co...]
    all_to_all x2, blocking collectives: 90.4 us -> 95 us  [the longest x1 79.8 us: on_device(): lax.all_to_all(payload, 'expert', split_axis=0, concat_axis=0, tiled=True)]
    convert_element_type x4 -> x1, other arithmetic: 4.58 us -> 0.83 us  [on_device(): gates = gate_values.T.astype(jnp.float32)]
    select_n x3 -> x0, other arithmetic: 3.68 us -> none  [the longest x1 2.16 us: on_device(): jnp.where(filled[:, :, None] > 0, grad_out[source_row], jnp.zeros((), gra...]
    reshape x1 -> x2, local copies, waits for them, and re-layouts: 3.49 us -> 7.13 us  [the longest x1 3.58 us: on_device(): landed = landed.reshape(slot_count, width + 128)]
  transfers between devices with their start and end apart: 2 -> 1, of which waited for: 2 -> 1; matrix products, arithmetic and copies ran while one was open for 1% -> 3% of each run, Pallas kernels for 0% -> 0%
where the time goes in v1:
time: 160 us; the launch traced here: 158 us
  blocking collectives  115 us (72%)
  between operations  14.1 us (9%)
  local copies, waits for them, and re-layouts  10.6 us (7%)
  matrix products  9.81 us (6%)
  other arithmetic  7.13 us (4%)
    all_to_all x1, blocking collectives, on_device(): lax.all_to_all(payload, 'expert', split_axis=0, concat_axis=0, tiled=True)  79.8 us
    psum x1, blocking collectives, on_device(): gate_total = lax.psum(gate_part, 'tensor')  19.7 us
    all_to_all x1, blocking collectives, on_device(): lax.all_to_all(gate_total.reshape(count, CAP), 'expert', split_axis=0, co...  15.3 us
    dot_general x1, matrix products, on_device(): lax.dot_general(arrived, scaled, (((0,), (0,)), ((), ())), preferred_elem...  4.46 us
    reshape x1, local copies, waits for them, and re-layouts, on_device(): landed = landed.reshape(slot_count, width + 128)  3.58 us
    reshape x1, local copies, waits for them, and re-layouts, on_device(): jnp.concatenate([outgoing, tail], axis=1).reshape(count, CAP, width + 128)  3.55 us
    dot_general x1, matrix products, on_device(): lax.dot_general(arrived, weight, (((1,), (1,)), ((), ())), preferred_elem...  3.37 us
  transfers between devices with their start and end apart: 1, of which 1 were waited for; matrix products, arithmetic and copies ran while one was open for 3% of the time, Pallas kernels for 0%

profile of v1, /device:TPU:1, one launch (start us, length us, event | category | flops | bytes accessed | tf_op | source)
XLA Modules:
  0.0 157.9 jit_solution(5118045864977009445)
XLA Ops:
  7.2 0.0 copy-start
  7.2 0.0 reduce-scatter.2.cloned.1.call-start
  7.2 0.8 convert_bitcast_fusion.1
  8.1 0.8 convert_reduce_fusion
  8.9 0.1 fusion.13
  9.0 0.1 eq.45
  9.1 0.1 select_reduce_fusion.3
  9.3 0.1 convert_element_type.53
  9.5 1.8 %convolution_convert_fusion.1 = bf16[192,4096]{1,0:T(8,128)(2,1)S(1)} fusion(bf16[128,4096]{1,0:T(8,128)(2,1)} %param.5, pred[192,128]{1,0:T(8,128)(4,1)S(1)} %bitcast.28, f32[192,128]{1,0:T(8,128)S(1)} %bitcast.27, f32[192]{0:T(256)S(1)} %eq.45), kind=kOutput, calls=%fused_computation.1 | convolution fusion | flops 202162176 | bytes 2745088 | tf_op jit(solution)/shard_map/dot_general | solution.py:30
  11.3 0.1 broadcast_in_dim.75
  11.4 1.3 pad_maximum_fusion
  12.7 3.5 %reshape.40 = bf16[48,4,4224]{2,1,0:T(4,128)(2,1)} reshape(bf16[192,4224]{1,0:T(8,128)(2,1)} %pad_maximum_fusion) | data formatting | bytes 3244032 | tf_op jit(solution)/shard_map/reshape | solution.py:36
  16.2 79.8 %all_to_all.14 = bf16[48,4,4224]{2,1,0:T(4,128)(2,1)} all-to-all(bf16[48,4,4224]{2,1,0:T(4,128)(2,1)} %reshape.40), channel_id=1, replica_groups=mesh['dp'=4,'expert'=48,'tensor'=4] {'expert'}, dimensions={0} | all-to-all | bytes 3244032 | tf_op jit(solution)/shard_map/all_to_all | solution.py:37
  96.0 0.0 copy-start.2
  96.0 3.6 %reshape.41 = bf16[192,4224]{1,0:T(8,128)(2,1)} reshape(bf16[48,4,4224]{2,1,0:T(4,128)(2,1)} %all_to_all.14) | data formatting | bytes 3244032 | tf_op jit(solution)/shard_map/reshape | solution.py:38
  99.6 0.9 convert_reduce_fusion.1
  100.5 0.0 copy-done.2
  100.5 4.5 %convolution_convert_fusion = bf16[4096,384]{1,0:T(8,128)(2,1)} fusion(bf16[192,4224]{1,0:T(8,128)(2,1)} %reshape.41, bf16[1,1,192,384]{3,2,1,0:T(8,128)(2,1)S(1)} %copy-done.2, f32[192]{0:T(256)S(1)} %convert_reduce_fusion.1), kind=kOutput, calls=%fused_computation | convolution fusion | flops 605773824 | bytes 4866816 | tf_op jit(solution)/shard_map/dot_general | solution.py:45
  105.0 0.0 reduce-scatter.2.cloned.1.call-update
  105.0 0.0 copy-done
  105.0 0.0 copy-start.1
  105.0 3.4 %fusion.6 = (bf16[1,1,192,384]{3,2,1,0:T(8,128)(2,1)}, f32[192]{0:T(256)S(1)}) fusion(f32[192]{0:T(256)S(1)} %convert_reduce_fusion.1, bf16[1,1,192,384]{3,2,1,0:T(8,128)(2,1)S(1)} %copy-done.2, bf16[1,384,4096]{2,1,0:T(8,128)(2,1)S(1)} %copy-done, bf16[192,4224]{1,0:T(8,128)(2,1)} %reshape.41), kind=kOutput, calls=%fused_computation.17 | convolution fusion | flops 604348224 | bytes 5015040 | tf_op jit(solution)/shard_map/dot_general | solution.py:50
  108.4 0.1 all_to_all.10
  108.5 19.7 %psum.7 = f32[48,1,4]{2,0,1:T(8,128)S(1)} all-reduce(f32[48,1,4]{2,0,1:T(8,128)S(1)} %all_to_all.10), channel_id=1, replica_groups=mesh['dp'=4,'expert'=48,'tensor'=4] {'tensor'}, use_global_device_ids=true, to_apply=%region_4.5 | all-reduce | flops 192 | bytes 1536 | tf_op jit(solution)/shard_map/psum | solution.py:55
  128.2 15.3 %all_to_all.15 = f32[48,1,4]{2,1,0:T(1,128)S(1)} all-to-all(f32[48,1,4]{2,1,0:T(1,128)S(1)} %bitcast.29), channel_id=1, replica_groups=mesh['dp'=4,'expert'=48,'tensor'=4] {'expert'}, dimensions={0} | all-to-all | bytes 1536 | tf_op jit(solution)/shard_map/all_to_all | solution.py:56
  143.4 0.1 select_reduce_fusion.2
  143.6 0.0 copy-done.1
  143.6 0.6 select_reduce_fusion
  144.2 1.4 reduce-scatter.2.cloned.1.call-done
  145.7 2.4 %convert_bitcast_fusion = f32[1,384,1024]{1,2,0:T(8,128)} fusion(bf16[1024,384]{1,0:T(8,128)(2,1)} %reduce-scatter.2.cloned.1.call-done), kind=kLoop, calls=%fused_computation.5 | loop fusion | flops 393216 | bytes 2359296 | tf_op jit(solution)/shard_map/broadcast_in_dim | solution.py:61
  148.0 3.0 %copy.22 = f32[1,384,1024]{2,1,0:T(8,128)} copy(f32[1,384,1024]{1,2,0:T(8,128)} %convert_bitcast_fusion) | data formatting | bytes 3145728
  (4 shorter events, 0.1 us)
Async XLA Ops:
  7.2 97.8 %copy-start = (bf16[1,384,4096]{2,1,0:T(8,128)(2,1)S(1)}, bf16[1,384,4096]{2,1,0:T(8,128)(2,1)}, u32[]{:S(2)}) copy-start(bf16[1,384,4096]{2,1,0:T(8,128)(2,1)} %param.9) | copy-start | bytes 9437188
  7.2 138.5 %reduce-scatter.2.cloned.1.call-start = ((), (), s32[]{:S(2)}) async-start(), calls=%async_computation.3 | async-start | bytes 3932160 | tf_op jit(solution)/shard_map/reduce_scatter | solution.py:44
  96.0 4.5 %copy-start.2 = (bf16[1,1,192,384]{3,2,1,0:T(8,128)(2,1)S(1)}, bf16[1,1,192,384]{3,2,1,0:T(8,128)(2,1)}, u32[]{:S(2)}) copy-start(bf16[1,1,192,384]{3,2,1,0:T(8,128)(2,1)} %param.8) | copy-start | bytes 442372
  105.0 38.6 %copy-start.1 = (s32[128,8]{0,1:T(8,128)S(1)}, s32[128,8]{0,1:T(8,128)}, u32[]{:S(2)}) copy-start(s32[128,8]{0,1:T(8,128)} %param.6) | copy-start | bytes 12292
Sparse Core Ops, SparseCore 0:
  105.1 40.4 reduce-scatter.1

commit v2 on v1

v2 whole, which is shorter than its diff:
```python
import jax
import jax.numpy as jnp
from jax import lax
from jax.experimental import pallas as pl
from jax.experimental.pallas import tpu as pltpu
from jax.sharding import PartitionSpec as P

CAP = 4
NZ = 12
NLO = 4
NX = 4
NT = 4
NE = NZ * NLO
GROUPS = 3
PER = NE // GROUPS
ROWS = PER * CAP
TOK = 128
LANE = 128
F32 = jnp.float32
BF16 = jnp.bfloat16
I32 = jnp.int32
MESH = pl.DeviceIdType.MESH


def offset_of(p):
    odd = p % 2
    return 6 + (1 - odd) * (p // 2) - odd * ((p + 1) // 2)


def iota(shape, dim):
    return lax.broadcasted_iota(I32, shape, dim)


def dot(a, b, dims=((1,), (0,))):
    return lax.dot_general(a, b, (dims, ((), ())), preferred_element_type=F32)


def kernel(ids_ref, gates_ref, grad_ref, hidden_ref, weight_ref,
           gg_ref, hg_ref, dw_ref,
           w_buf, pick_buf, g_buf, out_buf, in_buf, in2_buf,
           gout_buf, gin_buf, gate_buf, x_buf, xw_buf, xw2_buf, bw_buf, bw2_buf, h_buf,
           tout_buf, tin_buf, tsel_buf, part_buf, parts_buf,
           w_sem, own_sem, send_sem, a_sem, g_sem, h_sem, p1_sem, b_sem, p2_sem, t_sem, d_sem):
    x = lax.axis_index("dp")
    e = lax.axis_index("expert")
    t = lax.axis_index("tensor")
    z, lo = e // NLO, e % NLO
    hi, core = t // 2, t % 2

    def at_offset(dz, lo2):
        far = ((lo2 - lo) * (lo2 - lo)) // 9
        return {"dp": x, "expert": ((z + dz) % NZ) * NLO + lo2, "tensor": ((hi + far) % 2) * 2 + core}

    def x_peer(r):
        return {"dp": (x + r) % NX, "expert": e, "tensor": t}

    def t_peer(r):
        return {"dp": x, "expert": e, "tensor": (t + r) % NT}

    partner = {"dp": x, "expert": e, "tensor": hi * 2 + (1 - core)}

    barrier = pltpu.get_barrier_semaphore()

    def greet(p, carry):
        for lo2 in range(NLO):
            pl.semaphore_signal(barrier, inc=1, device_id=at_offset(offset_of(p), lo2), device_id_type=MESH)
        return carry

    lax.fori_loop(0, NZ - 1, greet, 0)
    for r in range(1, 4):
        pl.semaphore_signal(barrier, inc=1, device_id=at_offset(0, (lo + r) % NLO), device_id_type=MESH)
        pl.semaphore_signal(barrier, inc=1, device_id=x_peer(r), device_id_type=MESH)
        pl.semaphore_signal(barrier, inc=1, device_id=t_peer(r), device_id_type=MESH)

    w_copy = pltpu.make_async_copy(weight_ref, w_buf, w_sem)
    w_copy.start()

    row = iota((NE, TOK), 0)
    where_z = z + offset_of(row // NLO)
    expert = (where_z % NZ) * NLO + row % NLO
    member = jnp.zeros((NE, TOK), F32)
    gate = jnp.zeros((NE, TOK), F32)
    for k in range(8):
        hit = ids_ref[k:k + 1, :] == expert
        member = member + hit.astype(F32)
        gate = gate + jnp.where(hit, gates_ref[k:k + 1, :], 0.0)
    earlier = (iota((TOK, TOK), 0) < iota((TOK, TOK), 1)).astype(F32).astype(BF16)
    before = dot(member.astype(BF16), earlier)
    code = jnp.where((member > 0) & (before < CAP), before, -1.0)
    for c in range(CAP):
        picked = jnp.sum(jnp.where(code == c, gate, 0.0), axis=1, keepdims=True)
        wide = jnp.broadcast_to(picked, (NE, LANE))
        for s in range(NE):
            gout_buf[s, :, c * LANE:(c + 1) * LANE] = wide[s:s + 1, :]

    spread = (iota((NE * 16, NE), 0) // 16 == iota((NE * 16, NE), 1)).astype(F32).astype(BF16)
    code_wide = dot(spread, code.astype(BF16))
    place = iota((NE * 16, TOK), 0)
    chosen = code_wide == (place % CAP).astype(F32)
    part = (place // CAP) % 4
    for d in range(4):
        pick_buf[:, d * TOK:(d + 1) * TOK] = jnp.where(chosen & (part == d), 1.0, 0.0).astype(BF16)
    for q in range(4):
        for d in range(4):
            at = pl.multiple_of(q * 1024 + core * 512 + d * LANE, LANE)
            g_buf[d * TOK:(d + 1) * TOK, q * LANE:(q + 1) * LANE] = grad_ref[:, pl.ds(at, LANE)]
    for m in range(GROUPS):
        made = dot(pick_buf[m * 256:(m + 1) * 256, :], g_buf[...]).astype(BF16)
        for q in range(4):
            out_buf[q, m * 256:(m + 1) * 256, :] = made[:, q * LANE:(q + 1) * LANE]

    pl.semaphore_wait(barrier, 44 + 9)

    def block(ref, s):
        return ref.at[:, pl.ds(pl.multiple_of(s * 16, 16), 16), :]

    def send_rows(p, lo2, m):
        device = at_offset(offset_of(p), lo2)
        pltpu.make_async_remote_copy(
            src_ref=gout_buf.at[p * NLO + lo2], dst_ref=gin_buf.at[p * NLO + lo],
            send_sem=send_sem.at[1], recv_sem=g_sem.at[m], device_id=device, device_id_type=MESH).start()
        pltpu.make_async_remote_copy(
            src_ref=block(out_buf, p * NLO + lo2), dst_ref=block(in_buf, p * NLO + lo),
            send_sem=send_sem.at[0], recv_sem=a_sem.at[m], device_id=device, device_id_type=MESH).start()

    for m in range(GROUPS):
        def send_group(p, carry):
            for lo2 in range(NLO):
                send_rows(p, lo2, m)
            return carry

        lax.fori_loop(m * 4, m * 4 + (4 if m < 2 else 3), send_group, 0)
    for r in range(1, 4):
        send_rows(NZ - 1, (lo + r) % NLO, 2)
    mine = (NZ - 1) * NLO + lo
    pltpu.make_async_copy(block(out_buf, mine), block(in_buf, mine), a_sem.at[2]).start()
    pltpu.make_async_copy(gout_buf.at[mine], gin_buf.at[mine], g_sem.at[2]).start()
    for r in range(1, 4):
        pltpu.make_async_remote_copy(
            src_ref=hidden_ref, dst_ref=h_buf.at[r - 1],
            send_sem=send_sem.at[2], recv_sem=h_sem, device_id=x_peer(r), device_id_type=MESH).start()

    turn_row, turn_col = iota((256, 256), 0), iota((256, 256), 1)
    turn = ((turn_row // 64 == (turn_col // 4) % 4)
            & ((turn_row // 4) % 16 == turn_col // 16)
            & (turn_row % 4 == turn_col % 4)).astype(F32).astype(BF16)

    def natural(ref, m, xw, half):
        rows = jnp.concatenate([ref[q, m * 256:(m + 1) * 256, :] for q in range(4)], axis=1)
        turned = dot(turn, rows).astype(BF16)
        scale = gate_buf[...]
        for q in range(4):
            for d in range(4):
                piece = turned[d * ROWS:(d + 1) * ROWS, q * LANE:(q + 1) * LANE]
                at = pl.multiple_of(q * 1024 + half * 512 + d * LANE, LANE)
                x_buf[:, pl.ds(at, LANE)] = piece
                xw[m, q, :, d * LANE:(d + 1) * LANE] = (piece.astype(F32) * scale).astype(BF16)

    def wait_bytes(ref, sem):
        pltpu.make_async_copy(ref, ref, sem).wait()

    w_copy.wait()
    for m in range(GROUPS):
        rows = pl.ds(m * 256, 256)
        wait_bytes(in_buf.at[:, rows, :], a_sem.at[m])
        p1 = pltpu.make_async_remote_copy(
            src_ref=in_buf.at[:, rows, :], dst_ref=in2_buf.at[:, rows, :],
            send_sem=send_sem.at[3 + m], recv_sem=p1_sem.at[m], device_id=partner, device_id_type=MESH)
        p1.start()
        wait_bytes(gin_buf.at[pl.ds(m * PER, PER)], g_sem.at[m])
        for s in range(PER):
            for c in range(CAP):
                gate_buf[s * CAP + c:s * CAP + c + 1, :] = gin_buf[m * PER + s, :, c * LANE:(c + 1) * LANE]
        natural(in_buf, m, xw_buf, core)
        for r in range(1, 4):
            pltpu.make_async_remote_copy(
                src_ref=xw_buf.at[m, (x + r) % NX], dst_ref=bw_buf.at[m, r - 1],
                send_sem=send_sem.at[6 + m], recv_sem=b_sem.at[m], device_id=x_peer(r), device_id_type=MESH).start()
        p1.wait_recv()
        natural(in2_buf, m, xw2_buf, 1 - core)
        up = dot(x_buf[...], w_buf[...], ((1,), (1,)))
        wide_gate = jnp.concatenate([gate_buf[...]] * 3, axis=1)
        grads = (wide_gate * up).astype(BF16)
        for i in range(4):
            p = m * 4 + i
            at = pl.multiple_of(((z + NZ - offset_of(p)) % NZ) * 16, 16)
            hg_ref[pl.ds(at, 16), :] = grads[i * 16:(i + 1) * 16, :]
            rows16 = hidden_ref[pl.ds(at, 16), :]
            total = jnp.sum(rows16.astype(F32) * up[i * 16:(i + 1) * 16, :], axis=1, keepdims=True)
            wide = jnp.broadcast_to(total, (16, LANE))
            for s in range(4):
                for c in range(CAP):
                    tout_buf[p * NLO + s, :, c * LANE:(c + 1) * LANE] = wide[s * 4 + c:s * 4 + c + 1, :]

        def give_back(p, lo2):
            pltpu.make_async_remote_copy(
                src_ref=tout_buf.at[p * NLO + lo2], dst_ref=tin_buf.at[p * NLO + lo],
                send_sem=send_sem.at[9], recv_sem=t_sem,
                device_id=at_offset(NZ - offset_of(p), lo2), device_id_type=MESH).start()

        def back_group(p, carry):
            for lo2 in range(NLO):
                give_back(p, lo2)
            return carry

        lax.fori_loop(m * 4, m * 4 + (4 if m < 2 else 3), back_group, 0)
        if m == 2:
            for r in range(1, 4):
                give_back(NZ - 1, (lo + r) % NLO)
            pltpu.make_async_copy(tout_buf.at[mine], tin_buf.at[mine], t_sem).start()

        if m == 0:
            wait_bytes(h_buf, h_sem)
        wait_bytes(bw_buf.at[m], b_sem.at[m])
        p2 = pltpu.make_async_remote_copy(
            src_ref=bw_buf.at[m], dst_ref=bw2_buf.at[m],
            send_sem=send_sem.at[10 + m], recv_sem=p2_sem.at[m], device_id=partner, device_id_type=MESH)
        p2.start()
        pieces = []
        for i in range(4):
            at = pl.multiple_of(((z + NZ - offset_of(m * 4 + i)) % NZ) * 16, 16)
            pieces.append(at)
        held = jnp.concatenate(
            [hidden_ref[pl.ds(at, 16), :] for at in pieces]
            + [h_buf[r, pl.ds(at, 16), :] for r in range(3) for at in pieces], axis=0)
        first = jnp.concatenate([xw_buf[m, x]] + [bw_buf[m, r] for r in range(3)], axis=0)
        near = dot(held, first, ((0,), (0,)))
        lane0 = pl.ds(pl.multiple_of(core * 512, 512), 512)
        lane1 = pl.ds(pl.multiple_of((1 - core) * 512, 512), 512)
        dw_ref[:, lane0] = near if m == 0 else dw_ref[:, lane0] + near
        p2.wait_recv()
        second = jnp.concatenate([xw2_buf[m, x]] + [bw2_buf[m, r] for r in range(3)], axis=0)
        far_half = dot(held, second, ((0,), (0,)))
        dw_ref[:, lane1] = far_half if m == 0 else dw_ref[:, lane1] + far_half

    wait_bytes(tin_buf, t_sem)
    for s in range(NE):
        for c in range(CAP):
            tsel_buf[c, s:s + 1, :] = tin_buf[s, :, c * LANE:(c + 1) * LANE]
    value = jnp.zeros((NE, TOK), F32)
    for c in range(CAP):
        value = value + jnp.where(code == c, tsel_buf[c], 0.0)
    for k in range(8):
        hit = ids_ref[k:k + 1, :] == expert
        part_buf[k:k + 1, :] = jnp.sum(jnp.where(hit, value, 0.0), axis=0, keepdims=True)
    for r in range(1, 4):
        pltpu.make_async_remote_copy(
            src_ref=part_buf, dst_ref=parts_buf.at[r - 1],
            send_sem=send_sem.at[13], recv_sem=d_sem, device_id=t_peer(r), device_id_type=MESH).start()
    wait_bytes(parts_buf, d_sem)
    gg_ref[...] = (part_buf[...] + parts_buf[0]) + (parts_buf[1] + parts_buf[2])

    wait_bytes(out_buf.at[:, pl.ds(0, 47 * 16), :], send_sem.at[0])
    wait_bytes(gout_buf.at[pl.ds(0, 47)], send_sem.at[1])
    wait_bytes(h_buf, send_sem.at[2])
    for m in range(GROUPS):
        wait_bytes(in_buf.at[:, pl.ds(m * 256, 256), :], send_sem.at[3 + m])
        wait_bytes(bw_buf.at[m], send_sem.at[6 + m])
        wait_bytes(bw_buf.at[m], send_sem.at[10 + m])
    wait_bytes(tout_buf.at[pl.ds(0, 47)], send_sem.at[9])
    wait_bytes(parts_buf, send_sem.at[13])


def on_device(grad_out, expert_ids, gate_values, saved_hidden, down_weight):
    vmem = pl.BlockSpec(memory_space=pltpu.VMEM)
    dma = pltpu.SemaphoreType.DMA
    gg, hg, dw = pl.pallas_call(
        kernel,
        out_shape=(
            jax.ShapeDtypeStruct((8, TOK), F32),
            jax.ShapeDtypeStruct((192, 384), BF16),
            jax.ShapeDtypeStruct((384, 1024), F32),
        ),
        in_specs=[vmem, vmem, vmem, vmem, pl.BlockSpec(memory_space=pl.ANY)],
        out_specs=(vmem, vmem, vmem),
        scratch_shapes=[
            pltpu.VMEM((384, 4096), BF16),
            pltpu.VMEM((NE * 16, 512), BF16),
            pltpu.VMEM((512, 512), BF16),
            pltpu.VMEM((4, NE * 16, LANE), BF16),
            pltpu.VMEM((4, NE * 16, LANE), BF16),
            pltpu.VMEM((4, NE * 16, LANE), BF16),
            pltpu.VMEM((NE, 1, 512), F32),
            pltpu.VMEM((NE, 1, 512), F32),
            pltpu.VMEM((ROWS, LANE), F32),
            pltpu.VMEM((ROWS, 4096), BF16),
            pltpu.VMEM((GROUPS, 4, ROWS, 512), BF16),
            pltpu.VMEM((GROUPS, 4, ROWS, 512), BF16),
            pltpu.VMEM((GROUPS, 3, ROWS, 512), BF16),
            pltpu.VMEM((GROUPS, 3, ROWS, 512), BF16),
            pltpu.VMEM((3, 192, 384), BF16),
            pltpu.VMEM((NE, 1, 512), F32),
            pltpu.VMEM((NE, 1, 512), F32),
            pltpu.VMEM((CAP, NE, LANE), F32),
            pltpu.VMEM((8, TOK), F32),
            pltpu.VMEM((3, 8, TOK), F32),
            dma, dma, dma((14,)), dma((3,)), dma((3,)), dma, dma((3,)), dma((3,)), dma((3,)), dma, dma,
        ],
        compiler_params=pltpu.CompilerParams(
            collective_id=0, has_side_effects=True, vmem_limit_bytes=48 * 1024 * 1024
        ),
        name="exchange",
    )(expert_ids.T, gate_values.T.astype(F32), grad_out, saved_hidden[0, 0], down_weight[0])
    return (gg.T, hg[None, None], dw[None])


def solution(mesh):
    return jax.shard_map(
        on_device,
        mesh=mesh,
        in_specs=(
            P(("dp", "expert"), None),
            P(("dp", "expert"), None),
            P(("dp", "expert"), None),
            P("dp", "expert", None, "tensor"),
            P("expert", "tensor", None),
        ),
        out_specs=(
            P(("dp", "expert"), None),
            P("dp", "expert", None, "tensor"),
            P("expert", "tensor", "dp"),
        ),
        check_vma=False,
    )
```

time: 160 us -> 80.5 us (0.50); the launches traced: 158 us -> 80.2 us
  blocking collectives: 115 us -> 0 us
  Pallas kernels: 0 us -> 71.7 us
  between operations: 14.1 us -> 0.64 us
  matrix products: 9.81 us -> 0 us
  other arithmetic: 7.13 us -> 0.68 us
  local copies, waits for them, and re-layouts: 10.6 us -> 7.11 us
    all_to_all x2 -> x0, blocking collectives: 95 us -> none  [the longest x1 79.8 us: on_device(): lax.all_to_all(payload, 'expert', split_axis=0, concat_axis=0, tiled=True)]
    pallas_call x0 -> x1, Pallas kernels: none -> 71.7 us  [on_device(): pl.pallas_call(kernel, out_shape=(jax.ShapeDtypeStruct((8, TOK), F32), ja...]
    psum x1 -> x0, blocking collectives: 19.7 us -> none  [on_device(): gate_total = lax.psum(gate_part, 'tensor')]
    dot_general x4 -> x0, matrix products: 9.81 us -> none  [the longest x1 4.46 us: on_device(): lax.dot_general(arrived, scaled, (((0,), (0,)), ((), ())), preferred_elem...]
    reshape x2 -> x0, local copies, waits for them, and re-layouts: 7.13 us -> none  [the longest x1 3.58 us: on_device(): landed = landed.reshape(slot_count, width + 128)]
    unnamed x7 -> x11, local copies, waits for them, and re-layouts: 3.04 us -> 7.11 us
    broadcast_in_dim x1 -> x0, other arithmetic: 2.39 us -> none  [on_device(): down_grad = summed.astype(jnp.float32).T[None]]
    reduce_sum x4 -> x0, other arithmetic: 1.7 us -> none  [the longest x1 0.79 us: on_device(): member = jnp.sum(hits.astype(jnp.float32), axis=0)]
  transfers between devices with their start and end apart: 1 -> 0, of which waited for: 1 -> 0; matrix products, arithmetic and copies ran while one was open for 3% -> 0% of each run, Pallas kernels for 0% -> 0%
where the time goes in v2:
time: 80.5 us; the launch traced here: 80.2 us
  Pallas kernels  71.7 us (89%)
  local copies, waits for them, and re-layouts  7.11 us (9%)
    pallas_call x1, Pallas kernels, on_device(): pl.pallas_call(kernel, out_shape=(jax.ShapeDtypeStruct((8, TOK), F32), ja...  71.7 us
    unnamed x11, local copies, waits for them, and re-layouts  7.11 us

profile of v2, /device:TPU:1, one launch (start us, length us, event | category | flops | bytes accessed | tf_op | source)
XLA Modules:
  0.0 80.2 jit_solution(6016516864145153673)
XLA Ops:
  0.6 0.7 convert_bitcast_fusion.gates_ref
  1.3 0.0 copy-start
  1.3 1.9 %copy-done = bf16[1,384,4096]{2,1,0:T(8,128)(2,1)S(1)} copy-done((bf16[1,384,4096]{2,1,0:T(8,128)(2,1)S(1)}, bf16[1,384,4096]{2,1,0:T(8,128)(2,1)}, u32[]{:S(2)}) %copy-start) | copy-done | bytes 3145752
  3.2 0.0 copy-start.1
  3.2 1.2 %copy-done.1 = bf16[128,4096]{1,0:T(8,128)(2,1)S(1)} copy-done((bf16[128,4096]{1,0:T(8,128)(2,1)S(1)}, bf16[128,4096]{1,0:T(8,128)(2,1)}, u32[]{:S(2)}) %copy-start.1) | copy-done | bytes 1048600
  4.4 0.0 copy-start.2
  4.4 0.9 %copy-done.2 = bf16[1,1,192,384]{3,2,1,0:T(8,128)(2,1)S(1)} copy-done((bf16[1,1,192,384]{3,2,1,0:T(8,128)(2,1)S(1)}, bf16[1,1,192,384]{3,2,1,0:T(8,128)(2,1)}, u32[]{:S(2)}) %copy-start.2) | copy-done | bytes 147480
  5.3 0.0 copy-start.3
  5.3 0.7 copy-done.3
  6.0 71.7 %exchange.1 = (f32[8,128]{1,0:T(8,128)S(1)}, bf16[192,384]{1,0:T(8,128)(2,1)S(1)}, f32[384,1024]{1,0:T(8,128)S(1)}) custom-call(s32[8,128]{1,0:T(8,128)S(1)} %bitcast.13, f32[8,128]{1,0:T(8,128)S(1)} %convert_bitcast_fusion.gates_ref, bf16[128,4096]{1,0:T(8,128)(2,1)S(1)} %copy-done.1, bf16[192,384]{1,0:T(8,128)(2,1)S(1)} %bitcast.10, ...), custom_call_target="tpu_custom_call" | custom-call | tf_op jit(solution)/shard_map/exchange/pallas_call | solution.py:267
  77.8 0.6 copy.11
  78.4 0.7 copy.12
  79.0 1.1 %copy.13 = f32[1,384,1024]{2,1,0:T(8,128)} copy(f32[1,384,1024]{2,1,0:T(8,128)S(1)} %bitcast.9) | data formatting | bytes 3145728
Async XLA Ops:
  1.3 1.9 %copy-start = (bf16[1,384,4096]{2,1,0:T(8,128)(2,1)S(1)}, bf16[1,384,4096]{2,1,0:T(8,128)(2,1)}, u32[]{:S(2)}) copy-start(bf16[1,384,4096]{2,1,0:T(8,128)(2,1)} %param.9) | copy-start | bytes 9437188
  3.2 1.2 %copy-start.1 = (bf16[128,4096]{1,0:T(8,128)(2,1)S(1)}, bf16[128,4096]{1,0:T(8,128)(2,1)}, u32[]{:S(2)}) copy-start(bf16[128,4096]{1,0:T(8,128)(2,1)} %grad_ref.1) | copy-start | bytes 3145732
  4.4 0.9 %copy-start.2 = (bf16[1,1,192,384]{3,2,1,0:T(8,128)(2,1)S(1)}, bf16[1,1,192,384]{3,2,1,0:T(8,128)(2,1)}, u32[]{:S(2)}) copy-start(bf16[1,1,192,384]{3,2,1,0:T(8,128)(2,1)} %param.8) | copy-start | bytes 442372
  5.3 0.7 copy-start.3

commit v3 on v2

--- a/solution.py
+++ b/solution.py
@@ -35,20 +35,24 @@
     return lax.dot_general(a, b, (dims, ((), ())), preferred_element_type=F32)
 
 
-def kernel(ids_ref, gates_ref, grad_ref, hidden_ref, weight_ref,
+def crosses(a, b):
+    square = (b - a) * (b - a)
+    return square // 9 + ((square // 4) % 2) * ((a * (3 - a)) // 2)
+
+
+def kernel(ids_in, gates_in, grad_in, hidden_in, weight_ref,
            gg_ref, hg_ref, dw_ref,
-           w_buf, pick_buf, g_buf, out_buf, in_buf, in2_buf,
+           ids_ref, gates_ref, grad_ref, hidden_ref, w_buf, pick_buf, g_buf, out_buf, in_buf, in2_buf,
            gout_buf, gin_buf, gate_buf, x_buf, xw_buf, xw2_buf, bw_buf, bw2_buf, h_buf,
            tout_buf, tin_buf, tsel_buf, part_buf, parts_buf,
-           w_sem, own_sem, send_sem, a_sem, g_sem, h_sem, p1_sem, b_sem, p2_sem, t_sem, d_sem):
+           w_sem, load_sem, share_sem, send_sem, a_sem, g_sem, h_sem, p1_sem, b_sem, p2_sem, t_sem, d_sem):
     x = lax.axis_index("dp")
     e = lax.axis_index("expert")
     t = lax.axis_index("tensor")
     z, lo = e // NLO, e % NLO
     hi, core = t // 2, t % 2
 
-    def at_offset(dz, lo2):
-        far = ((lo2 - lo) * (lo2 - lo)) // 9
+    def at_offset(dz, lo2, far):
         return {"dp": x, "expert": ((z + dz) % NZ) * NLO + lo2, "tensor": ((hi + far) % 2) * 2 + core}
 
     def x_peer(r):
@@ -59,31 +63,44 @@
 
     partner = {"dp": x, "expert": e, "tensor": hi * 2 + (1 - core)}
 
+    loads = [pltpu.make_async_copy(a, b, load_sem.at[i]) for i, (a, b) in enumerate(
+        [(ids_in, ids_ref), (gates_in, gates_ref), (grad_in, grad_ref), (hidden_in, hidden_ref)])]
+    for load in loads:
+        load.start()
+    w_copy = pltpu.make_async_copy(weight_ref, w_buf, w_sem)
+    w_copy.start()
+
     barrier = pltpu.get_barrier_semaphore()
+    across = (lo + 2) % NLO
+
+    def greet_at(dz, lo2, far):
+        pl.semaphore_signal(barrier, inc=1, device_id=at_offset(dz, lo2, far), device_id_type=MESH)
 
     def greet(p, carry):
         for lo2 in range(NLO):
-            pl.semaphore_signal(barrier, inc=1, device_id=at_offset(offset_of(p), lo2), device_id_type=MESH)
+            greet_at(offset_of(p), lo2, crosses(lo, lo2))
+        greet_at(offset_of(p), across, crosses(across, lo))
         return carry
 
     lax.fori_loop(0, NZ - 1, greet, 0)
+    greet_at(0, across, crosses(across, lo))
     for r in range(1, 4):
-        pl.semaphore_signal(barrier, inc=1, device_id=at_offset(0, (lo + r) % NLO), device_id_type=MESH)
+        greet_at(0, (lo + r) % NLO, crosses(lo, (lo + r) % NLO))
         pl.semaphore_signal(barrier, inc=1, device_id=x_peer(r), device_id_type=MESH)
         pl.semaphore_signal(barrier, inc=1, device_id=t_peer(r), device_id_type=MESH)
-
-    w_copy = pltpu.make_async_copy(weight_ref, w_buf, w_sem)
-    w_copy.start()
 
     row = iota((NE, TOK), 0)
     where_z = z + offset_of(row // NLO)
     expert = (where_z % NZ) * NLO + row % NLO
     member = jnp.zeros((NE, TOK), F32)
     gate = jnp.zeros((NE, TOK), F32)
+    loads[0].wait()
+    loads[1].wait()
+    gate_rows = gates_ref[...].astype(F32)
     for k in range(8):
         hit = ids_ref[k:k + 1, :] == expert
         member = member + hit.astype(F32)
-        gate = gate + jnp.where(hit, gates_ref[k:k + 1, :], 0.0)
+        gate = gate + jnp.where(hit, gate_rows[k:k + 1, :], 0.0)
     earlier = (iota((TOK, TOK), 0) < iota((TOK, TOK), 1)).astype(F32).astype(BF16)
     before = dot(member.astype(BF16), earlier)
     code = jnp.where((member > 0) & (before < CAP), before, -1.0)
@@ -100,6 +117,7 @@
     part = (place // CAP) % 4
     for d in range(4):
         pick_buf[:, d * TOK:(d + 1) * TOK] = jnp.where(chosen & (part == d), 1.0, 0.0).astype(BF16)
+    loads[2].wait()
     for q in range(4):
         for d in range(4):
             at = pl.multiple_of(q * 1024 + core * 512 + d * LANE, LANE)
@@ -109,19 +127,21 @@
         for q in range(4):
             out_buf[q, m * 256:(m + 1) * 256, :] = made[:, q * LANE:(q + 1) * LANE]
 
-    pl.semaphore_wait(barrier, 44 + 9)
-
-    def block(ref, s):
-        return ref.at[:, pl.ds(pl.multiple_of(s * 16, 16), 16), :]
+    pl.semaphore_wait(barrier, 55 + 10)
+
+    def block(ref, s, planes=slice(None)):
+        return ref.at[planes, pl.ds(pl.multiple_of(s * 16, 16), 16), :]
 
     def send_rows(p, lo2, m):
-        device = at_offset(offset_of(p), lo2)
+        far = crosses(lo, lo2)
+        device = at_offset(offset_of(p), lo2, far)
+        planes = pl.ds(((hi + far) % 2) * 2, 2) if m == 0 else slice(None)
         pltpu.make_async_remote_copy(
             src_ref=gout_buf.at[p * NLO + lo2], dst_ref=gin_buf.at[p * NLO + lo],
             send_sem=send_sem.at[1], recv_sem=g_sem.at[m], device_id=device, device_id_type=MESH).start()
         pltpu.make_async_remote_copy(
-            src_ref=block(out_buf, p * NLO + lo2), dst_ref=block(in_buf, p * NLO + lo),
-            send_sem=send_sem.at[0], recv_sem=a_sem.at[m], device_id=device, device_id_type=MESH).start()
+            src_ref=block(out_buf, p * NLO + lo2, planes), dst_ref=block(in_buf, p * NLO + lo, planes),
+            send_sem=send_sem.at[0 if m == 0 else 14], recv_sem=a_sem.at[m], device_id=device, device_id_type=MESH).start()
 
     for m in range(GROUPS):
         def send_group(p, carry):
@@ -137,7 +157,7 @@
     pltpu.make_async_copy(gout_buf.at[mine], gin_buf.at[mine], g_sem.at[2]).start()
     for r in range(1, 4):
         pltpu.make_async_remote_copy(
-            src_ref=hidden_ref, dst_ref=h_buf.at[r - 1],
+            src_ref=hidden_in, dst_ref=h_buf.at[r - 1],
             send_sem=send_sem.at[2], recv_sem=h_sem, device_id=x_peer(r), device_id_type=MESH).start()
 
     turn_row, turn_col = iota((256, 256), 0), iota((256, 256), 1)
@@ -159,10 +179,20 @@
     def wait_bytes(ref, sem):
         pltpu.make_async_copy(ref, ref, sem).wait()
 
+    loads[3].wait()
     w_copy.wait()
     for m in range(GROUPS):
         rows = pl.ds(m * 256, 256)
-        wait_bytes(in_buf.at[:, rows, :], a_sem.at[m])
+        if m == 0:
+            got, lacking = pl.ds(hi * 2, 2), pl.ds((1 - hi) * 2, 2)
+            wait_bytes(in_buf.at[got, rows, :], a_sem.at[m])
+            share = pltpu.make_async_remote_copy(
+                src_ref=in_buf.at[got, rows, :], dst_ref=in_buf.at[got, rows, :],
+                send_sem=send_sem.at[15], recv_sem=share_sem, device_id=t_peer(2), device_id_type=MESH)
+            share.start()
+            wait_bytes(in_buf.at[lacking, rows, :], share_sem)
+        else:
+            wait_bytes(in_buf.at[:, rows, :], a_sem.at[m])
         p1 = pltpu.make_async_remote_copy(
             src_ref=in_buf.at[:, rows, :], dst_ref=in2_buf.at[:, rows, :],
             send_sem=send_sem.at[3 + m], recv_sem=p1_sem.at[m], device_id=partner, device_id_type=MESH)
@@ -196,7 +226,7 @@
             pltpu.make_async_remote_copy(
                 src_ref=tout_buf.at[p * NLO + lo2], dst_ref=tin_buf.at[p * NLO + lo],
                 send_sem=send_sem.at[9], recv_sem=t_sem,
-                device_id=at_offset(NZ - offset_of(p), lo2), device_id_type=MESH).start()
+                device_id=at_offset(NZ - offset_of(p), lo2, crosses(lo2, lo)), device_id_type=MESH).start()
 
         def back_group(p, carry):
             for lo2 in range(NLO):
@@ -250,7 +280,9 @@
     wait_bytes(parts_buf, d_sem)
     gg_ref[...] = (part_buf[...] + parts_buf[0]) + (parts_buf[1] + parts_buf[2])
 
-    wait_bytes(out_buf.at[:, pl.ds(0, 47 * 16), :], send_sem.at[0])
+    wait_bytes(out_buf.at[pl.ds(0, 2), pl.ds(0, 256), :], send_sem.at[0])
+    wait_bytes(out_buf.at[:, pl.ds(0, 31 * 16), :], send_sem.at[14])
+    wait_bytes(in_buf.at[pl.ds(0, 2), pl.ds(0, 256), :], send_sem.at[15])
     wait_bytes(gout_buf.at[pl.ds(0, 47)], send_sem.at[1])
     wait_bytes(h_buf, send_sem.at[2])
     for m in range(GROUPS):
@@ -261,19 +293,33 @@
     wait_bytes(parts_buf, send_sem.at[13])
 
 
+def flush(gg_ref, hg_ref, dw_ref, gg_out, hg_out, dw_out, sem):
+    moves = [pltpu.make_async_copy(a, b, sem.at[i]) for i, (a, b) in enumerate(
+        [(dw_ref, dw_out), (hg_ref, hg_out), (gg_ref, gg_out)])]
+    for move in moves:
+        move.start()
+    for move in moves:
+        move.wait()
+
+
 def on_device(grad_out, expert_ids, gate_values, saved_hidden, down_weight):
     vmem = pl.BlockSpec(memory_space=pltpu.VMEM)
+    hbm = pl.BlockSpec(memory_space=pltpu.HBM)
     dma = pltpu.SemaphoreType.DMA
     gg, hg, dw = pl.pallas_call(
         kernel,
         out_shape=(
-            jax.ShapeDtypeStruct((8, TOK), F32),
-            jax.ShapeDtypeStruct((192, 384), BF16),
-            jax.ShapeDtypeStruct((384, 1024), F32),
-        ),
-        in_specs=[vmem, vmem, vmem, vmem, pl.BlockSpec(memory_space=pl.ANY)],
+            pltpu.VMEM((8, TOK), F32),
+            pltpu.VMEM((192, 384), BF16),
+            pltpu.VMEM((384, 1024), F32),
+        ),
+        in_specs=[hbm] * 5,
         out_specs=(vmem, vmem, vmem),
         scratch_shapes=[
+            pltpu.VMEM((8, TOK), I32),
+            pltpu.VMEM((8, TOK), BF16),
+            pltpu.VMEM((TOK, 4096), BF16),
+            pltpu.VMEM((192, 384), BF16),
             pltpu.VMEM((384, 4096), BF16),
             pltpu.VMEM((NE * 16, 512), BF16),
             pltpu.VMEM((512, 512), BF16),
@@ -294,13 +340,26 @@
             pltpu.VMEM((CAP, NE, LANE), F32),
             pltpu.VMEM((8, TOK), F32),
             pltpu.VMEM((3, 8, TOK), F32),
-            dma, dma, dma((14,)), dma((3,)), dma((3,)), dma, dma((3,)), dma((3,)), dma((3,)), dma, dma,
+            dma, dma((4,)), dma, dma((16,)), dma((3,)), dma((3,)), dma, dma((3,)), dma((3,)), dma((3,)), dma, dma,
         ],
         compiler_params=pltpu.CompilerParams(
-            collective_id=0, has_side_effects=True, vmem_limit_bytes=48 * 1024 * 1024
+            collective_id=0, has_side_effects=True, vmem_limit_bytes=60 * 1024 * 1024
         ),
         name="exchange",
-    )(expert_ids.T, gate_values.T.astype(F32), grad_out, saved_hidden[0, 0], down_weight[0])
+    )(expert_ids.T, gate_values.T, grad_out, saved_hidden[0, 0], down_weight[0])
+    gg, hg, dw = pl.pallas_call(
+        flush,
+        out_shape=(
+            jax.ShapeDtypeStruct((8, TOK), F32),
+            jax.ShapeDtypeStruct((192, 384), BF16),
+            jax.ShapeDtypeStruct((384, 1024), F32),
+        ),
+        in_specs=[vmem] * 3,
+        out_specs=(hbm,) * 3,
+        scratch_shapes=[dma((3,))],
+        compiler_params=pltpu.CompilerParams(vmem_limit_bytes=1024 * 1024),
+        name="flush",
+    )(gg, hg, dw)
     return (gg.T, hg[None, None], dw[None])
 
 

time: 80.5 us -> 77.4 us (0.961)
  local copies, waits for them, and re-layouts: 7.11 us -> 0 us
  Pallas kernels: 71.7 us -> 76.6 us
    unnamed x11 -> x0, local copies, waits for them, and re-layouts: 7.11 us -> none
    pallas_call x1 -> x2, Pallas kernels: 71.7 us -> 76.6 us  [the longest x1 75.4 us: on_device(): pl.pallas_call(kernel, out_shape=(pltpu.VMEM((8, TOK), F32), pltpu.VMEM((...]
where the time goes in v3:
time: 77.4 us; the launch traced here: 77.3 us
  Pallas kernels  76.6 us (99%)
    pallas_call x1, Pallas kernels, on_device(): pl.pallas_call(kernel, out_shape=(pltpu.VMEM((8, TOK), F32), pltpu.VMEM((...  75.4 us

profile of v3, /device:TPU:1, one launch (start us, length us, event | category | flops | bytes accessed | tf_op | source)
XLA Modules:
  0.0 77.3 jit_solution(6017450497508996629)
XLA Ops:
  0.6 75.4 %exchange.1 = (f32[8,128]{1,0:T(8,128)S(1)}, bf16[192,384]{1,0:T(8,128)(2,1)S(1)}, f32[384,1024]{1,0:T(8,128)S(1)}) custom-call(s32[8,128]{1,0:T(8,128)} %bitcast.9, bf16[8,128]{1,0:T(8,128)(2,1)} %bitcast.10, bf16[128,4096]{1,0:T(8,128)(2,1)} %grad_in.1, bf16[192,384]{1,0:T(8,128)(2,1)} %bitcast.8, bf16[384,4096]{1,0:T(8,128)(2,1)} %bitcast.7), custom_call_target="tpu_custom_call" | custom-call | tf_op jit(solution)/shard_map/exchange/pallas_call | solution.py:309
  76.1 1.2 %flush.1 = (f32[8,128]{1,0:T(8,128)}, bf16[192,384]{1,0:T(8,128)(2,1)}, f32[384,1024]{1,0:T(8,128)}) custom-call(f32[8,128]{1,0:T(8,128)S(1)} %get-tuple-element.9.gg_ref, bf16[192,384]{1,0:T(8,128)(2,1)S(1)} %get-tuple-element.10.hg_ref, f32[384,1024]{1,0:T(8,128)S(1)} %get-tuple-element.11.dw_ref), custom_call_target="tpu_custom_call" | custom-call | tf_op jit(solution)/shard_map/flush/pallas_call | solution.py:350

commit v4 on v3

--- a/solution.py
+++ b/solution.py
@@ -22,7 +22,8 @@
 MESH = pl.DeviceIdType.MESH
 
 
-def offset_of(p):
+def offset_of(position):
+    p = (position + 8) % NZ
     odd = p % 2
     return 6 + (1 - odd) * (p // 2) - odd * ((p + 1) // 2)
 
@@ -71,23 +72,25 @@
     w_copy.start()
 
     barrier = pltpu.get_barrier_semaphore()
-    across = (lo + 2) % NLO
-
-    def greet_at(dz, lo2, far):
-        pl.semaphore_signal(barrier, inc=1, device_id=at_offset(dz, lo2, far), device_id_type=MESH)
-
-    def greet(p, carry):
+
+    def greet_at(dz, lo2, hi2):
+        pl.semaphore_signal(barrier, inc=1, device_id_type=MESH, device_id={
+            "dp": x, "expert": ((z + dz) % NZ) * NLO + lo2, "tensor": hi2 * 2 + core})
+
+    def greet(dz, carry):
         for lo2 in range(NLO):
-            greet_at(offset_of(p), lo2, crosses(lo, lo2))
-        greet_at(offset_of(p), across, crosses(across, lo))
+            for hi2 in range(2):
+                greet_at(dz, lo2, hi2)
         return carry
 
-    lax.fori_loop(0, NZ - 1, greet, 0)
-    greet_at(0, across, crosses(across, lo))
+    lax.fori_loop(1, NZ, greet, 0)
     for r in range(1, 4):
-        greet_at(0, (lo + r) % NLO, crosses(lo, (lo + r) % NLO))
+        for hi2 in range(2):
+            greet_at(0, (lo + r) % NLO, hi2)
+    greet_at(0, lo, 1 - hi)
+    pl.semaphore_signal(barrier, inc=1, device_id=partner, device_id_type=MESH)
+    for r in range(1, 4):
         pl.semaphore_signal(barrier, inc=1, device_id=x_peer(r), device_id_type=MESH)
-        pl.semaphore_signal(barrier, inc=1, device_id=t_peer(r), device_id_type=MESH)
 
     row = iota((NE, TOK), 0)
     where_z = z + offset_of(row // NLO)
@@ -127,7 +130,7 @@
         for q in range(4):
             out_buf[q, m * 256:(m + 1) * 256, :] = made[:, q * LANE:(q + 1) * LANE]
 
-    pl.semaphore_wait(barrier, 55 + 10)
+    pl.semaphore_wait(barrier, 95 + 4)
 
     def block(ref, s, planes=slice(None)):
         return ref.at[planes, pl.ds(pl.multiple_of(s * 16, 16), 16), :]
@@ -135,30 +138,37 @@
     def send_rows(p, lo2, m):
         far = crosses(lo, lo2)
         device = at_offset(offset_of(p), lo2, far)
-        planes = pl.ds(((hi + far) % 2) * 2, 2) if m == 0 else slice(None)
+        planes = pl.ds(((hi + far) % 2) * 2, 2) if m == 1 else slice(None)
+        rows_sem = a_sem.at[p] if m == 2 else a_sem.at[m]
         pltpu.make_async_remote_copy(
             src_ref=gout_buf.at[p * NLO + lo2], dst_ref=gin_buf.at[p * NLO + lo],
             send_sem=send_sem.at[1], recv_sem=g_sem.at[m], device_id=device, device_id_type=MESH).start()
         pltpu.make_async_remote_copy(
             src_ref=block(out_buf, p * NLO + lo2, planes), dst_ref=block(in_buf, p * NLO + lo, planes),
-            send_sem=send_sem.at[0 if m == 0 else 14], recv_sem=a_sem.at[m], device_id=device, device_id_type=MESH).start()
-
-    for m in range(GROUPS):
-        def send_group(p, carry):
+            send_sem=send_sem.at[0 if m == 1 else 14], recv_sem=rows_sem, device_id=device,
+            device_id_type=MESH).start()
+
+    def send_group(m):
+        def body(p, carry):
             for lo2 in range(NLO):
                 send_rows(p, lo2, m)
             return carry
-
-        lax.fori_loop(m * 4, m * 4 + (4 if m < 2 else 3), send_group, 0)
+        return body
+
+    mine = 3 * NLO + lo
+    lax.fori_loop(4, 8, send_group(1), 0)
     for r in range(1, 4):
-        send_rows(NZ - 1, (lo + r) % NLO, 2)
-    mine = (NZ - 1) * NLO + lo
-    pltpu.make_async_copy(block(out_buf, mine), block(in_buf, mine), a_sem.at[2]).start()
-    pltpu.make_async_copy(gout_buf.at[mine], gin_buf.at[mine], g_sem.at[2]).start()
+        send_rows(3, (lo + r) % NLO, 0)
+    lax.fori_loop(0, 3, send_group(0), 0)
+    pltpu.make_async_copy(block(out_buf, mine), block(in_buf, mine), a_sem.at[0]).start()
+    pltpu.make_async_copy(gout_buf.at[mine], gin_buf.at[mine], g_sem.at[0]).start()
     for r in range(1, 4):
         pltpu.make_async_remote_copy(
             src_ref=hidden_in, dst_ref=h_buf.at[r - 1],
             send_sem=send_sem.at[2], recv_sem=h_sem, device_id=x_peer(r), device_id_type=MESH).start()
+    for p in range(8, 12):
+        for lo2 in range(NLO):
+            send_rows(p, lo2, 2)
 
     turn_row, turn_col = iota((256, 256), 0), iota((256, 256), 1)
     turn = ((turn_row // 64 == (turn_col // 4) % 4)
@@ -179,24 +189,32 @@
     def wait_bytes(ref, sem):
         pltpu.make_async_copy(ref, ref, sem).wait()
 
-    loads[3].wait()
-    w_copy.wait()
-    for m in range(GROUPS):
+    def core_copy(m, rows):
+        return pltpu.make_async_remote_copy(
+            src_ref=in_buf.at[:, rows, :], dst_ref=in2_buf.at[:, rows, :],
+            send_sem=send_sem.at[3 + m], recv_sem=p1_sem.at[m], device_id=partner, device_id_type=MESH)
+
+    def rows_of(m):
+        return [pl.multiple_of(((z + NZ - offset_of(m * 4 + i)) % NZ) * 16, 16) for i in range(4)]
+
+    def take_rows(m):
         rows = pl.ds(m * 256, 256)
-        if m == 0:
+        if m == 2:
+            for p in range(8, 12):
+                part_rows = pl.ds(p * 64, 64)
+                wait_bytes(in_buf.at[:, part_rows, :], a_sem.at[p])
+                core_copy(m, part_rows).start()
+        elif m == 1:
             got, lacking = pl.ds(hi * 2, 2), pl.ds((1 - hi) * 2, 2)
             wait_bytes(in_buf.at[got, rows, :], a_sem.at[m])
-            share = pltpu.make_async_remote_copy(
+            pltpu.make_async_remote_copy(
                 src_ref=in_buf.at[got, rows, :], dst_ref=in_buf.at[got, rows, :],
-                send_sem=send_sem.at[15], recv_sem=share_sem, device_id=t_peer(2), device_id_type=MESH)
-            share.start()
+                send_sem=send_sem.at[15], recv_sem=share_sem, device_id=t_peer(2), device_id_type=MESH).start()
             wait_bytes(in_buf.at[lacking, rows, :], share_sem)
+            core_copy(m, rows).start()
         else:
             wait_bytes(in_buf.at[:, rows, :], a_sem.at[m])
-        p1 = pltpu.make_async_remote_copy(
-            src_ref=in_buf.at[:, rows, :], dst_ref=in2_buf.at[:, rows, :],
-            send_sem=send_sem.at[3 + m], recv_sem=p1_sem.at[m], device_id=partner, device_id_type=MESH)
-        p1.start()
+            core_copy(m, rows).start()
         wait_bytes(gin_buf.at[pl.ds(m * PER, PER)], g_sem.at[m])
         for s in range(PER):
             for c in range(CAP):
@@ -206,79 +224,98 @@
             pltpu.make_async_remote_copy(
                 src_ref=xw_buf.at[m, (x + r) % NX], dst_ref=bw_buf.at[m, r - 1],
                 send_sem=send_sem.at[6 + m], recv_sem=b_sem.at[m], device_id=x_peer(r), device_id_type=MESH).start()
-        p1.wait_recv()
+
+    def give_back(p, lo2):
+        for hi2 in range(2):
+            pltpu.make_async_remote_copy(
+                src_ref=tout_buf.at[p * NLO + lo2], dst_ref=tin_buf.at[hi, p * NLO + lo],
+                send_sem=send_sem.at[9 if hi2 == 0 else 16], recv_sem=t_sem, device_id_type=MESH, device_id={
+                    "dp": x, "expert": ((z + NZ - offset_of(p)) % NZ) * NLO + lo2,
+                    "tensor": hi2 * 2 + core}).start()
+
+    def back_group(p, carry):
+        for lo2 in range(NLO):
+            give_back(p, lo2)
+        return carry
+
+    def up_and_back(m):
+        wait_bytes(in2_buf.at[:, pl.ds(m * 256, 256), :], p1_sem.at[m])
         natural(in2_buf, m, xw2_buf, 1 - core)
         up = dot(x_buf[...], w_buf[...], ((1,), (1,)))
         wide_gate = jnp.concatenate([gate_buf[...]] * 3, axis=1)
         grads = (wide_gate * up).astype(BF16)
-        for i in range(4):
+        for i, at in enumerate(rows_of(m)):
             p = m * 4 + i
-            at = pl.multiple_of(((z + NZ - offset_of(p)) % NZ) * 16, 16)
-            hg_ref[pl.ds(at, 16), :] = grads[i * 16:(i + 1) * 16, :]
             rows16 = hidden_ref[pl.ds(at, 16), :]
             total = jnp.sum(rows16.astype(F32) * up[i * 16:(i + 1) * 16, :], axis=1, keepdims=True)
             wide = jnp.broadcast_to(total, (16, LANE))
             for s in range(4):
                 for c in range(CAP):
                     tout_buf[p * NLO + s, :, c * LANE:(c + 1) * LANE] = wide[s * 4 + c:s * 4 + c + 1, :]
-
-        def give_back(p, lo2):
+            hg_ref[pl.ds(at, 16), :] = grads[i * 16:(i + 1) * 16, :]
+        if m == 0:
+            for r in range(1, 4):
+                give_back(3, (lo + r) % NLO)
+            pltpu.make_async_copy(tout_buf.at[mine], tin_buf.at[hi, mine], t_sem).start()
             pltpu.make_async_remote_copy(
-                src_ref=tout_buf.at[p * NLO + lo2], dst_ref=tin_buf.at[p * NLO + lo],
-                send_sem=send_sem.at[9], recv_sem=t_sem,
-                device_id=at_offset(NZ - offset_of(p), lo2, crosses(lo2, lo)), device_id_type=MESH).start()
-
-        def back_group(p, carry):
-            for lo2 in range(NLO):
-                give_back(p, lo2)
-            return carry
-
-        lax.fori_loop(m * 4, m * 4 + (4 if m < 2 else 3), back_group, 0)
-        if m == 2:
-            for r in range(1, 4):
-                give_back(NZ - 1, (lo + r) % NLO)
-            pltpu.make_async_copy(tout_buf.at[mine], tin_buf.at[mine], t_sem).start()
-
-        if m == 0:
-            wait_bytes(h_buf, h_sem)
+                src_ref=tout_buf.at[mine], dst_ref=tin_buf.at[hi, mine],
+                send_sem=send_sem.at[17], recv_sem=t_sem, device_id=t_peer(2), device_id_type=MESH).start()
+        lax.fori_loop(m * 4, m * 4 + (3 if m == 0 else 4), back_group, 0)
+
+    def pass_on(m):
         wait_bytes(bw_buf.at[m], b_sem.at[m])
-        p2 = pltpu.make_async_remote_copy(
+        pltpu.make_async_remote_copy(
             src_ref=bw_buf.at[m], dst_ref=bw2_buf.at[m],
-            send_sem=send_sem.at[10 + m], recv_sem=p2_sem.at[m], device_id=partner, device_id_type=MESH)
-        p2.start()
-        pieces = []
-        for i in range(4):
-            at = pl.multiple_of(((z + NZ - offset_of(m * 4 + i)) % NZ) * 16, 16)
-            pieces.append(at)
+            send_sem=send_sem.at[10 + m], recv_sem=p2_sem.at[m], device_id=partner, device_id_type=MESH).start()
+
+    def contract(m):
+        at_rows = rows_of(m)
         held = jnp.concatenate(
-            [hidden_ref[pl.ds(at, 16), :] for at in pieces]
-            + [h_buf[r, pl.ds(at, 16), :] for r in range(3) for at in pieces], axis=0)
+            [hidden_ref[pl.ds(at, 16), :] for at in at_rows]
+            + [h_buf[r, pl.ds(at, 16), :] for r in range(3) for at in at_rows], axis=0)
         first = jnp.concatenate([xw_buf[m, x]] + [bw_buf[m, r] for r in range(3)], axis=0)
         near = dot(held, first, ((0,), (0,)))
         lane0 = pl.ds(pl.multiple_of(core * 512, 512), 512)
         lane1 = pl.ds(pl.multiple_of((1 - core) * 512, 512), 512)
         dw_ref[:, lane0] = near if m == 0 else dw_ref[:, lane0] + near
-        p2.wait_recv()
+        wait_bytes(bw2_buf.at[m], p2_sem.at[m])
         second = jnp.concatenate([xw2_buf[m, x]] + [bw2_buf[m, r] for r in range(3)], axis=0)
         far_half = dot(held, second, ((0,), (0,)))
         dw_ref[:, lane1] = far_half if m == 0 else dw_ref[:, lane1] + far_half
 
+    loads[3].wait()
+    w_copy.wait()
+    take_rows(0)
+    up_and_back(0)
+    pass_on(0)
+    take_rows(1)
+    up_and_back(1)
+    wait_bytes(h_buf, h_sem)
+    contract(0)
+    pass_on(1)
+    take_rows(2)
+    up_and_back(2)
+    contract(1)
+    pass_on(2)
+    contract(2)
+
     wait_bytes(tin_buf, t_sem)
     for s in range(NE):
         for c in range(CAP):
-            tsel_buf[c, s:s + 1, :] = tin_buf[s, :, c * LANE:(c + 1) * LANE]
+            lanes = slice(c * LANE, (c + 1) * LANE)
+            tsel_buf[c, s:s + 1, :] = tin_buf[0, s, :, lanes] + tin_buf[1, s, :, lanes]
     value = jnp.zeros((NE, TOK), F32)
     for c in range(CAP):
         value = value + jnp.where(code == c, tsel_buf[c], 0.0)
     for k in range(8):
         hit = ids_ref[k:k + 1, :] == expert
         part_buf[k:k + 1, :] = jnp.sum(jnp.where(hit, value, 0.0), axis=0, keepdims=True)
-    for r in range(1, 4):
-        pltpu.make_async_remote_copy(
-            src_ref=part_buf, dst_ref=parts_buf.at[r - 1],
-            send_sem=send_sem.at[13], recv_sem=d_sem, device_id=t_peer(r), device_id_type=MESH).start()
-    wait_bytes(parts_buf, d_sem)
-    gg_ref[...] = (part_buf[...] + parts_buf[0]) + (parts_buf[1] + parts_buf[2])
+    last = pltpu.make_async_remote_copy(
+        src_ref=part_buf, dst_ref=parts_buf,
+        send_sem=send_sem.at[13], recv_sem=d_sem, device_id=partner, device_id_type=MESH)
+    last.start()
+    last.wait()
+    gg_ref[...] = part_buf[...] + parts_buf[...]
 
     wait_bytes(out_buf.at[pl.ds(0, 2), pl.ds(0, 256), :], send_sem.at[0])
     wait_bytes(out_buf.at[:, pl.ds(0, 31 * 16), :], send_sem.at[14])
@@ -290,7 +327,8 @@
         wait_bytes(bw_buf.at[m], send_sem.at[6 + m])
         wait_bytes(bw_buf.at[m], send_sem.at[10 + m])
     wait_bytes(tout_buf.at[pl.ds(0, 47)], send_sem.at[9])
-    wait_bytes(parts_buf, send_sem.at[13])
+    wait_bytes(tout_buf.at[pl.ds(0, 47)], send_sem.at[16])
+    wait_bytes(tout_buf.at[0], send_sem.at[17])
 
 
 def flush(gg_ref, hg_ref, dw_ref, gg_out, hg_out, dw_out, sem):
@@ -336,11 +374,11 @@
             pltpu.VMEM((GROUPS, 3, ROWS, 512), BF16),
             pltpu.VMEM((3, 192, 384), BF16),
             pltpu.VMEM((NE, 1, 512), F32),
-            pltpu.VMEM((NE, 1, 512), F32),
+            pltpu.VMEM((2, NE, 1, 512), F32),
             pltpu.VMEM((CAP, NE, LANE), F32),
             pltpu.VMEM((8, TOK), F32),
-            pltpu.VMEM((3, 8, TOK), F32),
-            dma, dma((4,)), dma, dma((16,)), dma((3,)), dma((3,)), dma, dma((3,)), dma((3,)), dma((3,)), dma, dma,
+            pltpu.VMEM((8, TOK), F32),
+            dma, dma((4,)), dma, dma((18,)), dma((12,)), dma((3,)), dma, dma((3,)), dma((3,)), dma((3,)), dma, dma,
         ],
         compiler_params=pltpu.CompilerParams(
             collective_id=0, has_side_effects=True, vmem_limit_bytes=60 * 1024 * 1024

time: 77.4 us -> 71.1 us (0.919)
  Pallas kernels: 76.6 us -> 70.3 us
    pallas_call x1, Pallas kernels: 75.4 us -> 69.1 us  [on_device(): pl.pallas_call(kernel, out_shape=(pltpu.VMEM((8, TOK), F32), pltpu.VMEM((...]
where the time goes in v4:
time: 71.1 us; the launch traced here: 71 us
  Pallas kernels  70.3 us (99%)
    pallas_call x1, Pallas kernels, on_device(): pl.pallas_call(kernel, out_shape=(pltpu.VMEM((8, TOK), F32), pltpu.VMEM((...  69.1 us

profile of v4, /device:TPU:1, one launch (start us, length us, event | category | flops | bytes accessed | tf_op | source)
XLA Modules:
  0.0 71.0 jit_solution(17110418487475725748)
XLA Ops:
  0.6 69.1 %exchange.1 = (f32[8,128]{1,0:T(8,128)S(1)}, bf16[192,384]{1,0:T(8,128)(2,1)S(1)}, f32[384,1024]{1,0:T(8,128)S(1)}) custom-call(s32[8,128]{1,0:T(8,128)} %bitcast.9, bf16[8,128]{1,0:T(8,128)(2,1)} %bitcast.10, bf16[128,4096]{1,0:T(8,128)(2,1)} %grad_in.1, bf16[192,384]{1,0:T(8,128)(2,1)} %bitcast.8, bf16[384,4096]{1,0:T(8,128)(2,1)} %bitcast.7), custom_call_target="tpu_custom_call" | custom-call | tf_op jit(solution)/shard_map/exchange/pallas_call | solution.py:347
  69.7 1.2 %flush.1 = (f32[8,128]{1,0:T(8,128)}, bf16[192,384]{1,0:T(8,128)(2,1)}, f32[384,1024]{1,0:T(8,128)}) custom-call(f32[8,128]{1,0:T(8,128)S(1)} %get-tuple-element.9.gg_ref, bf16[192,384]{1,0:T(8,128)(2,1)S(1)} %get-tuple-element.10.hg_ref, f32[384,1024]{1,0:T(8,128)S(1)} %get-tuple-element.11.dw_ref), custom_call_target="tpu_custom_call" | custom-call | tf_op jit(solution)/shard_map/flush/pallas_call | solution.py:388

commit v5 on v4

--- a/solution.py
+++ b/solution.py
@@ -68,8 +68,11 @@
         [(ids_in, ids_ref), (gates_in, gates_ref), (grad_in, grad_ref), (hidden_in, hidden_ref)])]
     for load in loads:
         load.start()
-    w_copy = pltpu.make_async_copy(weight_ref, w_buf, w_sem)
-    w_copy.start()
+    for half in range(2):
+        for q in range(4):
+            at = pl.multiple_of(q * 1024 + ((core + half) % 2) * 512, 512)
+            pltpu.make_async_copy(
+                weight_ref.at[:, pl.ds(at, 512)], w_buf.at[half, :, pl.ds(q * 512, 512)], w_sem).start()
 
     barrier = pltpu.get_barrier_semaphore()
 
@@ -107,11 +110,13 @@
     earlier = (iota((TOK, TOK), 0) < iota((TOK, TOK), 1)).astype(F32).astype(BF16)
     before = dot(member.astype(BF16), earlier)
     code = jnp.where((member > 0) & (before < CAP), before, -1.0)
+    lane = iota((NE, LANE), 1)
+    sent_gates = jnp.zeros((NE, LANE), F32)
     for c in range(CAP):
         picked = jnp.sum(jnp.where(code == c, gate, 0.0), axis=1, keepdims=True)
-        wide = jnp.broadcast_to(picked, (NE, LANE))
-        for s in range(NE):
-            gout_buf[s, :, c * LANE:(c + 1) * LANE] = wide[s:s + 1, :]
+        sent_gates = jnp.where(lane == c, picked, sent_gates)
+    for s in range(NE):
+        gout_buf[s] = sent_gates[s:s + 1, :]
 
     spread = (iota((NE * 16, NE), 0) // 16 == iota((NE * 16, NE), 1)).astype(F32).astype(BF16)
     code_wide = dot(spread, code.astype(BF16))
@@ -175,19 +180,21 @@
             & ((turn_row // 4) % 16 == turn_col // 16)
             & (turn_row % 4 == turn_col % 4)).astype(F32).astype(BF16)
 
-    def natural(ref, m, xw, half):
+    def natural(ref, m, xw):
         rows = jnp.concatenate([ref[q, m * 256:(m + 1) * 256, :] for q in range(4)], axis=1)
         turned = dot(turn, rows).astype(BF16)
         scale = gate_buf[...]
         for q in range(4):
             for d in range(4):
                 piece = turned[d * ROWS:(d + 1) * ROWS, q * LANE:(q + 1) * LANE]
-                at = pl.multiple_of(q * 1024 + half * 512 + d * LANE, LANE)
-                x_buf[:, pl.ds(at, LANE)] = piece
+                at = q * 512 + d * LANE
+                x_buf[:, at:at + LANE] = piece
                 xw[m, q, :, d * LANE:(d + 1) * LANE] = (piece.astype(F32) * scale).astype(BF16)
 
     def wait_bytes(ref, sem):
         pltpu.make_async_copy(ref, ref, sem).wait()
+
+    own_lane = iota((ROWS, LANE), 1) == iota((ROWS, LANE), 0) % CAP
 
     def core_copy(m, rows):
         return pltpu.make_async_remote_copy(
@@ -218,49 +225,53 @@
         wait_bytes(gin_buf.at[pl.ds(m * PER, PER)], g_sem.at[m])
         for s in range(PER):
             for c in range(CAP):
-                gate_buf[s * CAP + c:s * CAP + c + 1, :] = gin_buf[m * PER + s, :, c * LANE:(c + 1) * LANE]
-        natural(in_buf, m, xw_buf, core)
+                gate_buf[s * CAP + c:s * CAP + c + 1, :] = gin_buf[m * PER + s]
+        column = jnp.sum(jnp.where(own_lane, gate_buf[...], 0.0), axis=1, keepdims=True)
+        gate_buf[...] = jnp.broadcast_to(column, (ROWS, LANE))
+        natural(in_buf, m, xw_buf)
         for r in range(1, 4):
             pltpu.make_async_remote_copy(
                 src_ref=xw_buf.at[m, (x + r) % NX], dst_ref=bw_buf.at[m, r - 1],
                 send_sem=send_sem.at[6 + m], recv_sem=b_sem.at[m], device_id=x_peer(r), device_id_type=MESH).start()
-
-    def give_back(p, lo2):
+        return dot(x_buf[...], w_buf[0], ((1,), (1,)))
+
+    def give_back(p, lo2, m):
         for hi2 in range(2):
             pltpu.make_async_remote_copy(
                 src_ref=tout_buf.at[p * NLO + lo2], dst_ref=tin_buf.at[hi, p * NLO + lo],
-                send_sem=send_sem.at[9 if hi2 == 0 else 16], recv_sem=t_sem, device_id_type=MESH, device_id={
+                send_sem=send_sem.at[9 if hi2 == 0 else 16], recv_sem=t_sem.at[m], device_id_type=MESH, device_id={
                     "dp": x, "expert": ((z + NZ - offset_of(p)) % NZ) * NLO + lo2,
                     "tensor": hi2 * 2 + core}).start()
 
-    def back_group(p, carry):
-        for lo2 in range(NLO):
-            give_back(p, lo2)
-        return carry
-
-    def up_and_back(m):
+    def back_group(m):
+        def body(p, carry):
+            for lo2 in range(NLO):
+                give_back(p, lo2, m)
+            return carry
+        return body
+
+    def up_and_back(m, up_own):
         wait_bytes(in2_buf.at[:, pl.ds(m * 256, 256), :], p1_sem.at[m])
-        natural(in2_buf, m, xw2_buf, 1 - core)
-        up = dot(x_buf[...], w_buf[...], ((1,), (1,)))
+        natural(in2_buf, m, xw2_buf)
+        up = up_own + dot(x_buf[...], w_buf[1], ((1,), (1,)))
         wide_gate = jnp.concatenate([gate_buf[...]] * 3, axis=1)
         grads = (wide_gate * up).astype(BF16)
         for i, at in enumerate(rows_of(m)):
             p = m * 4 + i
             rows16 = hidden_ref[pl.ds(at, 16), :]
             total = jnp.sum(rows16.astype(F32) * up[i * 16:(i + 1) * 16, :], axis=1, keepdims=True)
-            wide = jnp.broadcast_to(total, (16, LANE))
+            wide = jnp.where(own_lane[:16], total, 0.0)
             for s in range(4):
-                for c in range(CAP):
-                    tout_buf[p * NLO + s, :, c * LANE:(c + 1) * LANE] = wide[s * 4 + c:s * 4 + c + 1, :]
+                tout_buf[p * NLO + s] = jnp.sum(wide[s * 4:s * 4 + 4, :], axis=0, keepdims=True)
             hg_ref[pl.ds(at, 16), :] = grads[i * 16:(i + 1) * 16, :]
         if m == 0:
             for r in range(1, 4):
-                give_back(3, (lo + r) % NLO)
-            pltpu.make_async_copy(tout_buf.at[mine], tin_buf.at[hi, mine], t_sem).start()
+                give_back(3, (lo + r) % NLO, 0)
+            pltpu.make_async_copy(tout_buf.at[mine], tin_buf.at[hi, mine], t_sem.at[0]).start()
             pltpu.make_async_remote_copy(
                 src_ref=tout_buf.at[mine], dst_ref=tin_buf.at[hi, mine],
-                send_sem=send_sem.at[17], recv_sem=t_sem, device_id=t_peer(2), device_id_type=MESH).start()
-        lax.fori_loop(m * 4, m * 4 + (3 if m == 0 else 4), back_group, 0)
+                send_sem=send_sem.at[17], recv_sem=t_sem.at[0], device_id=t_peer(2), device_id_type=MESH).start()
+        lax.fori_loop(m * 4, m * 4 + (3 if m == 0 else 4), back_group(m), 0)
 
     def pass_on(m):
         wait_bytes(bw_buf.at[m], b_sem.at[m])
@@ -284,29 +295,26 @@
         dw_ref[:, lane1] = far_half if m == 0 else dw_ref[:, lane1] + far_half
 
     loads[3].wait()
-    w_copy.wait()
-    take_rows(0)
-    up_and_back(0)
+    wait_bytes(w_buf, w_sem)
+    up_and_back(0, take_rows(0))
     pass_on(0)
-    take_rows(1)
-    up_and_back(1)
+    up_and_back(1, take_rows(1))
     wait_bytes(h_buf, h_sem)
     contract(0)
     pass_on(1)
-    take_rows(2)
-    up_and_back(2)
+    up_and_back(2, take_rows(2))
     contract(1)
     pass_on(2)
     contract(2)
 
-    wait_bytes(tin_buf, t_sem)
-    for s in range(NE):
-        for c in range(CAP):
-            lanes = slice(c * LANE, (c + 1) * LANE)
-            tsel_buf[c, s:s + 1, :] = tin_buf[0, s, :, lanes] + tin_buf[1, s, :, lanes]
+    for m in range(GROUPS):
+        wait_bytes(tin_buf.at[:, pl.ds(m * PER, PER)], t_sem.at[m])
+        for s in range(m * PER, (m + 1) * PER):
+            tsel_buf[s:s + 1, :] = tin_buf[0, s] + tin_buf[1, s]
     value = jnp.zeros((NE, TOK), F32)
     for c in range(CAP):
-        value = value + jnp.where(code == c, tsel_buf[c], 0.0)
+        column = jnp.sum(jnp.where(lane == c, tsel_buf[...], 0.0), axis=1, keepdims=True)
+        value = jnp.where(code == c, column, value)
     for k in range(8):
         hit = ids_ref[k:k + 1, :] == expert
         part_buf[k:k + 1, :] = jnp.sum(jnp.where(hit, value, 0.0), axis=0, keepdims=True)
@@ -358,27 +366,27 @@
             pltpu.VMEM((8, TOK), BF16),
             pltpu.VMEM((TOK, 4096), BF16),
             pltpu.VMEM((192, 384), BF16),
-            pltpu.VMEM((384, 4096), BF16),
+            pltpu.VMEM((2, 384, 2048), BF16),
             pltpu.VMEM((NE * 16, 512), BF16),
             pltpu.VMEM((512, 512), BF16),
             pltpu.VMEM((4, NE * 16, LANE), BF16),
             pltpu.VMEM((4, NE * 16, LANE), BF16),
             pltpu.VMEM((4, NE * 16, LANE), BF16),
-            pltpu.VMEM((NE, 1, 512), F32),
-            pltpu.VMEM((NE, 1, 512), F32),
+            pltpu.VMEM((NE, 1, LANE), F32),
+            pltpu.VMEM((NE, 1, LANE), F32),
             pltpu.VMEM((ROWS, LANE), F32),
-            pltpu.VMEM((ROWS, 4096), BF16),
+            pltpu.VMEM((ROWS, 2048), BF16),
             pltpu.VMEM((GROUPS, 4, ROWS, 512), BF16),
             pltpu.VMEM((GROUPS, 4, ROWS, 512), BF16),
             pltpu.VMEM((GROUPS, 3, ROWS, 512), BF16),
             pltpu.VMEM((GROUPS, 3, ROWS, 512), BF16),
             pltpu.VMEM((3, 192, 384), BF16),
-            pltpu.VMEM((NE, 1, 512), F32),
-            pltpu.VMEM((2, NE, 1, 512), F32),
-            pltpu.VMEM((CAP, NE, LANE), F32),
+            pltpu.VMEM((NE, 1, LANE), F32),
+            pltpu.VMEM((2, NE, 1, LANE), F32),
+            pltpu.VMEM((NE, LANE), F32),
             pltpu.VMEM((8, TOK), F32),
             pltpu.VMEM((8, TOK), F32),
-            dma, dma((4,)), dma, dma((18,)), dma((12,)), dma((3,)), dma, dma((3,)), dma((3,)), dma((3,)), dma, dma,
+            dma, dma((4,)), dma, dma((18,)), dma((12,)), dma((3,)), dma, dma((3,)), dma((3,)), dma((3,)), dma((3,)), dma,
         ],
         compiler_params=pltpu.CompilerParams(
             collective_id=0, has_side_effects=True, vmem_limit_bytes=60 * 1024 * 1024

time: 71.1 us -> 68.7 us (0.966)
  Pallas kernels: 70.3 us -> 67.9 us
    pallas_call x1, Pallas kernels: 69.1 us -> 66.7 us  [on_device(): pl.pallas_call(kernel, out_shape=(pltpu.VMEM((8, TOK), F32), pltpu.VMEM((...]
where the time goes in v5:
time: 68.7 us; the launch traced here: 68.5 us
  Pallas kernels  67.9 us (99%)
    pallas_call x1, Pallas kernels, on_device(): pl.pallas_call(kernel, out_shape=(pltpu.VMEM((8, TOK), F32), pltpu.VMEM((...  66.7 us

profile of v5, /device:TPU:1, one launch (start us, length us, event | category | flops | bytes accessed | tf_op | source)
XLA Modules:
  0.0 68.5 jit_solution(11201830674292938853)
XLA Ops:
  0.6 66.7 %exchange.1 = (f32[8,128]{1,0:T(8,128)S(1)}, bf16[192,384]{1,0:T(8,128)(2,1)S(1)}, f32[384,1024]{1,0:T(8,128)S(1)}) custom-call(s32[8,128]{1,0:T(8,128)} %bitcast.9, bf16[8,128]{1,0:T(8,128)(2,1)} %bitcast.10, bf16[128,4096]{1,0:T(8,128)(2,1)} %grad_in.1, bf16[192,384]{1,0:T(8,128)(2,1)} %bitcast.8, bf16[384,4096]{1,0:T(8,128)(2,1)} %bitcast.7), custom_call_target="tpu_custom_call" | custom-call | tf_op jit(solution)/shard_map/exchange/pallas_call | solution.py:355
  67.3 1.2 %flush.1 = (f32[8,128]{1,0:T(8,128)}, bf16[192,384]{1,0:T(8,128)(2,1)}, f32[384,1024]{1,0:T(8,128)}) custom-call(f32[8,128]{1,0:T(8,128)S(1)} %get-tuple-element.9.gg_ref, bf16[192,384]{1,0:T(8,128)(2,1)S(1)} %get-tuple-element.10.hg_ref, f32[384,1024]{1,0:T(8,128)S(1)} %get-tuple-element.11.dw_ref), custom_call_target="tpu_custom_call" | custom-call | tf_op jit(solution)/shard_map/flush/pallas_call | solution.py:396

commit v6 on v5

--- a/solution.py
+++ b/solution.py
@@ -171,8 +171,8 @@
         pltpu.make_async_remote_copy(
             src_ref=hidden_in, dst_ref=h_buf.at[r - 1],
             send_sem=send_sem.at[2], recv_sem=h_sem, device_id=x_peer(r), device_id_type=MESH).start()
-    for p in range(8, 12):
-        for lo2 in range(NLO):
+    for lo2 in range(NLO):
+        for p in range(8, 12):
             send_rows(p, lo2, 2)
 
     turn_row, turn_col = iota((256, 256), 0), iota((256, 256), 1)
@@ -299,10 +299,11 @@
     up_and_back(0, take_rows(0))
     pass_on(0)
     up_and_back(1, take_rows(1))
+    up_own = take_rows(2)
+    pass_on(1)
+    up_and_back(2, up_own)
     wait_bytes(h_buf, h_sem)
     contract(0)
-    pass_on(1)
-    up_and_back(2, take_rows(2))
     contract(1)
     pass_on(2)
     contract(2)

time: 68.7 us -> 66.7 us (0.971)
  Pallas kernels: 67.9 us -> 65.9 us
    pallas_call x1, Pallas kernels: 66.7 us -> 64.7 us  [on_device(): pl.pallas_call(kernel, out_shape=(pltpu.VMEM((8, TOK), F32), pltpu.VMEM((...]
where the time goes in v6:
time: 66.7 us; the launch traced here: 66.5 us
  Pallas kernels  65.9 us (99%)
    pallas_call x1, Pallas kernels, on_device(): pl.pallas_call(kernel, out_shape=(pltpu.VMEM((8, TOK), F32), pltpu.VMEM((...  64.7 us

profile of v6, /device:TPU:1, one launch (start us, length us, event | category | flops | bytes accessed | tf_op | source)
XLA Modules:
  0.0 66.5 jit_solution(15911713647114910649)
XLA Ops:
  0.6 64.7 %exchange.1 = (f32[8,128]{1,0:T(8,128)S(1)}, bf16[192,384]{1,0:T(8,128)(2,1)S(1)}, f32[384,1024]{1,0:T(8,128)S(1)}) custom-call(s32[8,128]{1,0:T(8,128)} %bitcast.9, bf16[8,128]{1,0:T(8,128)(2,1)} %bitcast.10, bf16[128,4096]{1,0:T(8,128)(2,1)} %grad_in.1, bf16[192,384]{1,0:T(8,128)(2,1)} %bitcast.8, bf16[384,4096]{1,0:T(8,128)(2,1)} %bitcast.7), custom_call_target="tpu_custom_call" | custom-call | tf_op jit(solution)/shard_map/exchange/pallas_call | solution.py:356
  65.3 1.2 %flush.1 = (f32[8,128]{1,0:T(8,128)}, bf16[192,384]{1,0:T(8,128)(2,1)}, f32[384,1024]{1,0:T(8,128)}) custom-call(f32[8,128]{1,0:T(8,128)S(1)} %get-tuple-element.9.gg_ref, bf16[192,384]{1,0:T(8,128)(2,1)S(1)} %get-tuple-element.10.hg_ref, f32[384,1024]{1,0:T(8,128)S(1)} %get-tuple-element.11.dw_ref), custom_call_target="tpu_custom_call" | custom-call | tf_op jit(solution)/shard_map/flush/pallas_call | solution.py:397
